TPU v7x, 256 devices: a whole 4x4x8 slice. The times are simulated.
256 devices in a mesh: gx: 16 (over x, y), gy: 16 (over z, core).
Axes of the slice: x: 4, y: 4, z: 8, core: 2. Of those that a mesh axis runs over, the one named last changes fastest.
Arguments:
- initial_value: float32 [64, 128, 1024], P('gx', 'gy'), may hold values from -3.5 to 3.5
- disturbance: float32 [64, 128], P('gx', 'gy'), may hold values from 0.05 to 4.4
Outputs:
- final_value: float32 [64, 128, 1024], P('gx', 'gy')
All inputs are finite; a program needn't handle non-finite values.
Results may differ from a plain program's by a relative error of at most 0.00002.
Values sent between devices are 32-bit elements; how exact they have to be, the bound alone decides.
A program may use at most 64 MiB of HBM per device.

v0:
```python
import functools
import math

import jax
import jax.numpy as jnp
from jax import lax
from jax.sharding import Mesh
from jax.sharding import PartitionSpec as P

HEADINGS = 16
SPEEDS = 16
TURNS = 4
GX = ("gx_0", "gx_1")
GY = ("gy_0", "gy_1")
GX_GY = ("gx_0", "gx_1", "gy_0", "gy_1")


step_xy = 0.1
step_speed = 0.1
step_turn = 0.1
speed_low = 1.0
accel = 0.5
torque = 0.3
courant = 0.75
smooth_eps = 1e-06
radius_eps = 0.01


def with_halo(block, sides, width):
    for axis, dim in sides:
        count = lax.axis_size(axis)
        forward = [(i, i + 1) for i in range(count - 1)]
        backward = [(target, source) for source, target in forward]
        low = lax.ppermute(
            lax.slice_in_dim(block, block.shape[dim] - width, None, axis=dim), axis, forward
        )
        high = lax.ppermute(lax.slice_in_dim(block, 0, width, axis=dim), axis, backward)
        block = jnp.concatenate([low, block, high], axis=dim)
    return block


def by_axis(array, axes):
    return functools.reduce(lax.pmax, axes, array)


def ghosts(grid_values, along):
    width = grid_values.shape[along]
    first = lax.slice_in_dim(grid_values, 0, 1, axis=along)
    second = lax.slice_in_dim(grid_values, 1, 2, axis=along)
    last_row = lax.slice_in_dim(grid_values, width - 1, width, axis=along)
    before_last = lax.slice_in_dim(grid_values, width - 2, width - 1, axis=along)
    left_side = [first + factor * (first - second) for factor in (3.0, 2.0, 1.0)]
    right_side = [last_row + factor * (last_row - before_last) for factor in (1.0, 2.0, 3.0)]
    return jnp.concatenate(left_side + [grid_values] + right_side, axis=along)


def border_fix(extended, grid_values, along, at_start, at_end):
    extrapolated = ghosts(grid_values, along)
    length = extended.shape[along]
    view_shape = [1] * extended.ndim
    view_shape[along] = length
    position = jnp.arange(length, dtype=jnp.int32).reshape(view_shape)
    outside = at_start & (position < 3) | at_end & (position >= length - 3)
    return jnp.where(outside, extrapolated, extended)


def axis_shifts(extended, along, length_out):
    return [
        lax.slice_in_dim(extended, 3 + offset, 3 + offset + length_out, axis=along)
        for offset in range(-3, 4)
    ]


def flat_shifts(grid_values, stride, extent, periodic):
    lanes_here = grid_values.shape[-1]
    position = jnp.arange(lanes_here, dtype=jnp.int32) // stride % extent

    def rolled(offset):
        return jnp.roll(grid_values, -offset * stride, axis=-1)

    result = []
    for offset in range(-3, 4):
        target = position + offset
        shifted = rolled(offset)
        if offset != 0:
            if periodic:
                wrapped = rolled(offset - extent if offset > 0 else offset + extent)
                shifted = jnp.where((target >= 0) & (target < extent), shifted, wrapped)
            else:
                for beyond in range(1, abs(offset) + 1):
                    if offset > 0:
                        edge_cell = rolled(offset - beyond)
                        inner_cell = rolled(offset - beyond - 1)
                        struck = target == extent - 1 + beyond
                    else:
                        edge_cell = rolled(offset + beyond)
                        inner_cell = rolled(offset + beyond + 1)
                        struck = target == -beyond
                    shifted = jnp.where(
                        struck, edge_cell + beyond * (edge_cell - inner_cell), shifted
                    )
        result.append(shifted)
    return result


def weno_side(slope_a, slope_b, slope_c, slope_d, slope_e):
    guess_one = slope_a / 3.0 - 7.0 * slope_b / 6.0 + 11.0 * slope_c / 6.0
    guess_two = -slope_b / 6.0 + 5.0 * slope_c / 6.0 + slope_d / 3.0
    guess_three = slope_c / 3.0 + 5.0 * slope_d / 6.0 - slope_e / 6.0
    rough_one = (
        13.0 / 12.0 * (slope_a - 2.0 * slope_b + slope_c) ** 2
        + 0.25 * (slope_a - 4.0 * slope_b + 3.0 * slope_c) ** 2
    )
    rough_two = (
        13.0 / 12.0 * (slope_b - 2.0 * slope_c + slope_d) ** 2 + 0.25 * (slope_b - slope_d) ** 2
    )
    rough_three = (
        13.0 / 12.0 * (slope_c - 2.0 * slope_d + slope_e) ** 2
        + 0.25 * (3.0 * slope_c - 4.0 * slope_d + slope_e) ** 2
    )
    weight_one = 0.1 / (rough_one + smooth_eps) ** 2
    weight_two = 0.6 / (rough_two + smooth_eps) ** 2
    weight_three = 0.3 / (rough_three + smooth_eps) ** 2
    return (weight_one * guess_one + weight_two * guess_two + weight_three * guess_three) / (
        weight_one + weight_two + weight_three
    )


def weno(shifted, spacing):
    differ = [(shifted[offset + 1] - shifted[offset]) / spacing for offset in range(6)]
    left_slope = weno_side(differ[0], differ[1], differ[2], differ[3], differ[4])
    right_slope = weno_side(differ[5], differ[4], differ[3], differ[2], differ[1])
    return (left_slope, right_slope)


def flat_slopes(grid_values):
    return [
        weno(flat_shifts(grid_values, 1, HEADINGS, True), 2.0 * math.pi / HEADINGS),
        weno(flat_shifts(grid_values, HEADINGS, SPEEDS, False), step_speed),
        weno(flat_shifts(grid_values, HEADINGS * SPEEDS, TURNS, False), step_turn),
    ]


def lane_coords(lanes_here):
    lanes_all = jnp.arange(lanes_here, dtype=jnp.int32)
    heading = -math.pi + ((lanes_all % HEADINGS).astype(jnp.float32) + 0.5) * (
        2.0 * math.pi / HEADINGS
    )
    speed = speed_low + step_speed * (lanes_all // HEADINGS % SPEEDS).astype(jnp.float32)
    turning = step_turn * (
        (lanes_all // (HEADINGS * SPEEDS)).astype(jnp.float32) - (TURNS - 1) / 2.0
    )
    return (speed * jnp.cos(heading), speed * jnp.sin(heading), turning)


def centered(slopes):
    return [(one_sided[0] + one_sided[1]) * 0.5 for one_sided in slopes]


def speed_bounds(means, disturb_cells, coords):
    radius = jnp.sqrt(means[0] * means[0] + means[1] * means[1] + radius_eps)
    bound_x = jnp.abs(coords[0] - disturb_cells * means[0] / radius)
    bound_y = jnp.abs(coords[1] - disturb_cells * means[1] / radius)
    return (jnp.max(bound_x), jnp.max(bound_y))


def change_rate(slopes, means, disturb_cells, coords, alpha_x, alpha_y):
    radius = jnp.sqrt(means[0] * means[0] + means[1] * means[1] + radius_eps)
    hamilton = means[0] * coords[0] + means[1] * coords[1] + means[2] * coords[2]
    hamilton = (
        hamilton + accel * jnp.abs(means[3]) + torque * jnp.abs(means[4]) - disturb_cells * radius
    )
    turn_peak = step_turn * (TURNS - 1) / 2.0
    for coefficient, one_sided in zip((alpha_x, alpha_y, turn_peak, accel, torque), slopes):
        hamilton = hamilton - coefficient * (one_sided[1] - one_sided[0]) * 0.5
    return -hamilton


def time_step(alpha_x, alpha_y):
    turn_peak = step_turn * (TURNS - 1) / 2.0
    total = alpha_x / step_xy + alpha_y / step_xy + turn_peak / (2.0 * math.pi / HEADINGS)
    return courant / (total + accel / step_speed + torque / step_turn)


def body(initial_value, disturbance):
    row_start = lax.axis_index(GX) == 0
    row_end = lax.axis_index(GX) == lax.axis_size(GX) - 1
    column_start = lax.axis_index(GY) == 0
    column_end = lax.axis_index(GY) == lax.axis_size(GY) - 1
    coords = lane_coords(initial_value.shape[-1])
    disturb_cells = disturbance[:, :, None]

    def slopes_of(grid_values):
        rows_here = grid_values.shape[0]
        columns_here = grid_values.shape[1]
        along_rows = with_halo(grid_values, ((GX, 0),), 3)
        along_columns = with_halo(grid_values, ((GY, 1),), 3)
        along_rows = border_fix(along_rows, grid_values, 0, row_start, row_end)
        along_columns = border_fix(along_columns, grid_values, 1, column_start, column_end)
        return [
            weno(axis_shifts(along_rows, 0, rows_here), step_xy),
            weno(axis_shifts(along_columns, 1, columns_here), step_xy),
        ] + flat_slopes(grid_values)

    def section_maxima(means):
        peak_x, peak_y = speed_bounds(means, disturb_cells, coords)
        return (by_axis(peak_x, GX_GY), by_axis(peak_y, GX_GY))

    current = initial_value
    slopes = slopes_of(current)
    means = centered(slopes)
    start_x, start_y = speed_bounds(means, disturb_cells, coords)
    alpha_x, alpha_y = (by_axis(start_x, GX_GY), by_axis(start_y, GX_GY))
    for sweep_index in range(2):
        time_delta = time_step(alpha_x, alpha_y)
        if sweep_index > 0:
            slopes = slopes_of(current)
            means = centered(slopes)
        first_section = current + time_delta * change_rate(
            slopes, means, disturb_cells, coords, alpha_x, alpha_y
        )
        slopes = slopes_of(first_section)
        means = centered(slopes)
        if sweep_index == 0:
            peaks_two = section_maxima(means)
        second_section = 0.75 * current + 0.25 * (
            first_section
            + time_delta * change_rate(slopes, means, disturb_cells, coords, alpha_x, alpha_y)
        )
        slopes = slopes_of(second_section)
        means = centered(slopes)
        if sweep_index == 0:
            peaks_three = section_maxima(means)
        next_value = current / 3.0 + 2.0 / 3.0 * (
            second_section
            + time_delta * change_rate(slopes, means, disturb_cells, coords, alpha_x, alpha_y)
        )
        if sweep_index == 0:
            merged_x = jnp.maximum(peaks_two[0], peaks_three[0])
            merged_y = jnp.maximum(peaks_two[1], peaks_three[1])
            alpha_x, alpha_y = (merged_x, merged_y)
        current = next_value
    return current


def solution(mesh):
    torus = Mesh(mesh.devices.reshape(4, 4, 8, 2), ("gx_0", "gx_1", "gy_0", "gy_1"))
    placed = (P(GX, GY, None), P(GX, GY))
    return jax.shard_map(
        body, mesh=torus, in_specs=placed, out_specs=P(GX, GY, None), check_vma=False
    )
```

profile of v0, /device:TPU:99, one launch (start us, length us, event | category | flops | bytes accessed | tf_op | source)
XLA Modules:
  0.0 400.9 jit_solution(9973480564456670093)
XLA Ops:
  1.8 3.3 collective-permute-start
  5.1 4.2 %collective-permute-start.1 = (f32[3,8,1024]{2,0,1:T(4,128)}, f32[3,8,1024]{2,0,1:T(4,128)}, u32[]{:S(2)}, u32[]{:S(2)}) collective-permute-start(f32[3,8,1024]{2,0,1:T(4,128)} %get-tuple-element.353), channel_id=1, source_target_pairs={{16,0},{32,16},{48,32},{64,48},{80,64},{96,80},{112,96},{128,112},... | collective-permute-start | bytes 294920 | tf_op jit(solution)/shard_map/ppermute | solution.py:37
  9.9 5.9 %collective-permute-start.2 = (f32[4,3,1024]{2,0,1:T(4,128)}, f32[4,3,1024]{2,0,1:T(4,128)}, u32[]{:S(2)}, u32[]{:S(2)}) collective-permute-start(f32[4,3,1024]{2,0,1:T(4,128)} %get-tuple-element.350), channel_id=1, source_target_pairs={{0,1},{1,2},{2,3},{3,4},{4,5},{5,6},{6,7},{7,8},{8,9},{9,10},{10,1... | collective-permute-start | bytes 147464 | tf_op jit(solution)/shard_map/ppermute | solution.py:34
  15.8 1.9 collective-permute-start.3
  38.2 1.9 concatenate.660
  42.4 3.6 abs_reduce_fusion.5
  46.0 7.3 %all-reduce.5 = (f32[]{:T(128)}, f32[]{:T(128)}) all-reduce(f32[]{:T(128)} %get-tuple-element.10, f32[]{:T(128)} %get-tuple-element.9), channel_id=1, replica_groups=mesh['gx_0'=4,'gx_1'=4,'gy_0'=8,'gy_1'=2] {'gx_0'}, use_global_device_ids=true, to_apply=%region_6.7 | all-reduce | flops 2 | bytes 16 | tf_op jit(solution)/shard_map/pmax | solution.py:43
  53.3 7.5 %all-reduce.3 = (f32[]{:T(128)}, f32[]{:T(128)}) all-reduce(f32[]{:T(128)} %get-tuple-element.23, f32[]{:T(128)} %get-tuple-element.24), channel_id=1, replica_groups=mesh['gx_0'=4,'gx_1'=4,'gy_0'=8,'gy_1'=2] {'gx_1'}, use_global_device_ids=true, to_apply=%region_7.8 | all-reduce | flops 2 | bytes 16 | tf_op jit(solution)/shard_map/pmax | solution.py:43
  60.7 11.2 %all-reduce.1 = (f32[]{:T(128)}, f32[]{:T(128)}) all-reduce(f32[]{:T(128)} %get-tuple-element.19, f32[]{:T(128)} %get-tuple-element.20), channel_id=1, replica_groups=mesh['gx_0'=4,'gx_1'=4,'gy_0'=8,'gy_1'=2] {'gy_0'}, use_global_device_ids=true, to_apply=%region_8.9 | all-reduce | flops 2 | bytes 16 | tf_op jit(solution)/shard_map/pmax | solution.py:43
  71.9 12.4 %all-reduce.7 = (f32[]{:T(128)}, f32[]{:T(128)}) all-reduce(f32[]{:T(128)} %get-tuple-element.15, f32[]{:T(128)} %get-tuple-element.16), channel_id=1, replica_groups=mesh['gx_0'=4,'gx_1'=4,'gy_0'=8,'gy_1'=2] {'gy_1'}, use_global_device_ids=true, to_apply=%region_9.10 | all-reduce | flops 2 | bytes 16 | tf_op jit(solution)/shard_map/pmax | solution.py:43
  86.6 9.7 %multiply_add_fusion.51 = f32[4,8,1024]{2,0,1:T(4,128)S(1)} fusion(f32[4,8,1024]{2,0,1:T(4,128)S(1)} %get-tuple-element.41, f32[4,8,1024]{2,0,1:T(4,128)S(1)} %get-tuple-element.40, f32[4,8,1024]{2,0,1:T(4,128)S(1)} %get-tuple-element.39, f32[4,8,1024]{2,0,1:T(4,128)S(1)} %get-tuple-element.38, f32[4,8,256]{2,0,1:T(4,128)S(1)} %get-tuple-element.345, ...), kind=kLoop, calls=%fused_computation.1233 | loop fusion | flops 18120704 | bytes 3582092 | tf_op jit(solution)/shard_map/add | solution.py:219
  106.7 3.1 collective-permute-start.6
  109.8 1.9 collective-permute-start.7
  111.7 2.7 collective-permute-start.4
  114.5 4.8 %collective-permute-start.5 = (f32[3,8,1024]{2,0,1:T(4,128)S(1)}, f32[3,8,1024]{2,0,1:T(4,128)}, u32[]{:S(2)}, u32[]{:S(2)}) collective-permute-start(f32[3,8,1024]{2,0,1:T(4,128)S(1)} %get-tuple-element.259), channel_id=1, source_target_pairs={{16,0},{32,16},{48,32},{64,48},{80,64},{96,80},{112,96},{128,112},... | collective-permute-start | bytes 294920 | tf_op jit(solution)/shard_map/ppermute | solution.py:37
  123.9 22.3 %multiply_add_fusion.42 = (f32[4,8,1024]{2,0,1:T(4,128)S(1)}, f32[4,8,1024]{2,0,1:T(4,128)S(1)}, f32[4,8,1024]{2,0,1:T(4,128)S(1)}, f32[4,8,1024]{2,0,1:T(4,128)S(1)}, f32[4,8,1024]{2,0,1:T(4,128)S(1)}) fusion(f32[4,8,1024]{2,0,1:T(4,128)S(1)} %multiply_add_fusion.51, f32[4,8,256]{2,0,1:T(4,128)S(1)} %get-tuple-element.303, f32[4,8,768]{2,0,1:T(4,128)S(1)} %copy-done.8, ...), kind=kLoop, calls=%fused_computation.1039 | loop fusion | flops 27131904 | bytes 5548172 | tf_op jit(solution)/shard_map/add | solution.py:226
  158.5 5.4 %collective-permute-start.10 = (f32[4,3,1024]{2,0,1:T(4,128)}, f32[4,3,1024]{2,0,1:T(4,128)}, u32[]{:S(2)}, u32[]{:S(2)}) collective-permute-start(f32[4,3,1024]{2,0,1:T(4,128)} %get-tuple-element.246), channel_id=1, source_target_pairs={{0,1},{1,2},{2,3},{3,4},{4,5},{5,6},{6,7},{7,8},{8,9},{9,10},{10,1... | collective-permute-start | bytes 147464 | tf_op jit(solution)/shard_map/ppermute | solution.py:34
  163.9 1.9 collective-permute-start.11
  165.9 1.9 collective-permute-start.8
  167.8 6.3 %collective-permute-start.9 = (f32[3,8,1024]{2,0,1:T(4,128)S(1)}, f32[3,8,1024]{2,0,1:T(4,128)}, u32[]{:S(2)}, u32[]{:S(2)}) collective-permute-start(f32[3,8,1024]{2,0,1:T(4,128)S(1)} %get-tuple-element.249), channel_id=1, source_target_pairs={{16,0},{32,16},{48,32},{64,48},{80,64},{96,80},{112,96},{128,112},... | collective-permute-start | bytes 294920 | tf_op jit(solution)/shard_map/ppermute | solution.py:37
  174.1 1.9 concatenate.710
  179.4 3.8 abs_reduce_fusion.3
  184.0 9.6 %multiply_add_fusion.33 = f32[4,8,1024]{2,0,1:T(4,128)S(1)} fusion(f32[4,8,1024]{2,0,1:T(4,128)S(1)} %get-tuple-element.33, f32[4,8,1024]{2,0,1:T(4,128)S(1)} %get-tuple-element.32, f32[4,8,1024]{2,0,1:T(4,128)S(1)} %get-tuple-element.31, f32[4,8,1024]{2,0,1:T(4,128)S(1)} %get-tuple-element.30, f32[4,8,1024]{2,0,1:T(4,128)S(1)} %get-tuple-element.29, ...), kind=kLoop, calls=%fused_computation.845 | loop fusion | flops 18219008 | bytes 3713164 | tf_op jit(solution)/shard_map/add | solution.py:234
  207.0 7.5 %all-reduce.4 = (f32[]{:T(128)}, f32[]{:T(128)}) all-reduce(f32[]{:T(128)S(6)} %max.55, f32[]{:T(128)S(6)} %max.54), channel_id=1, replica_groups=mesh['gx_0'=4,'gx_1'=4,'gy_0'=8,'gy_1'=2] {'gx_0'}, use_global_device_ids=true, to_apply=%region_21.22 | all-reduce | flops 2 | bytes 16 | tf_op jit(solution)/shard_map/pmax | solution.py:43
  214.5 10.3 %all-reduce.2 = (f32[]{:T(128)}, f32[]{:T(128)}) all-reduce(f32[]{:T(128)} %get-tuple-element.21, f32[]{:T(128)} %get-tuple-element.22), channel_id=1, replica_groups=mesh['gx_0'=4,'gx_1'=4,'gy_0'=8,'gy_1'=2] {'gx_1'}, use_global_device_ids=true, to_apply=%region_22.23 | all-reduce | flops 2 | bytes 16 | tf_op jit(solution)/shard_map/pmax | solution.py:43
  224.8 11.1 %all-reduce = (f32[]{:T(128)}, f32[]{:T(128)}) all-reduce(f32[]{:T(128)} %get-tuple-element.17, f32[]{:T(128)} %get-tuple-element.18), channel_id=1, replica_groups=mesh['gx_0'=4,'gx_1'=4,'gy_0'=8,'gy_1'=2] {'gy_0'}, use_global_device_ids=true, to_apply=%region_23.24 | all-reduce | flops 2 | bytes 16 | tf_op jit(solution)/shard_map/pmax | solution.py:43
  236.0 12.3 %all-reduce.6 = (f32[]{:T(128)}, f32[]{:T(128)}) all-reduce(f32[]{:T(128)} %get-tuple-element.13, f32[]{:T(128)} %get-tuple-element.14), channel_id=1, replica_groups=mesh['gx_0'=4,'gx_1'=4,'gy_0'=8,'gy_1'=2] {'gy_1'}, use_global_device_ids=true, to_apply=%region_24.25 | all-reduce | flops 2 | bytes 16 | tf_op jit(solution)/shard_map/pmax | solution.py:43
  249.7 1.9 collective-permute-start.12
  251.6 5.5 %collective-permute-start.13 = (f32[3,8,1024]{2,0,1:T(4,128)}, f32[3,8,1024]{2,0,1:T(4,128)}, u32[]{:S(2)}, u32[]{:S(2)}) collective-permute-start(f32[3,8,1024]{2,0,1:T(4,128)} %get-tuple-element.153), channel_id=1, source_target_pairs={{16,0},{32,16},{48,32},{64,48},{80,64},{96,80},{112,96},{128,112},... | collective-permute-start | bytes 294920 | tf_op jit(solution)/shard_map/ppermute | solution.py:37
  257.2 4.5 %collective-permute-start.14 = (f32[4,3,1024]{2,0,1:T(4,128)}, f32[4,3,1024]{2,0,1:T(4,128)}, u32[]{:S(2)}, u32[]{:S(2)}) collective-permute-start(f32[4,3,1024]{2,0,1:T(4,128)} %get-tuple-element.160), channel_id=1, source_target_pairs={{0,1},{1,2},{2,3},{3,4},{4,5},{5,6},{6,7},{7,8},{8,9},{9,10},{10,1... | collective-permute-start | bytes 147464 | tf_op jit(solution)/shard_map/ppermute | solution.py:34
  261.7 1.9 collective-permute-start.15
  263.6 1.9 concatenate.735
  265.6 3.0 collective-permute-done.15
  272.0 22.3 %multiply_add_fusion.22 = f32[4,8,1024]{2,0,1:T(4,128)S(1)} fusion(f32[4,8,1024]{2,0,1:T(4,128)S(1)} %multiply_add_fusion.33, f32[4,8,256]{2,0,1:T(4,128)S(1)} %copy-done.18, f32[4,8,768]{2,0,1:T(4,128)S(1)} %get-tuple-element.201, f32[4,8,512]{2,0,1:T(4,128)S(1)} %copy-done.14, f32[4,8,512]{2,0,1:T(4,128)S(1)} %get-tuple-element.202, ...), kind=kLoop, calls=%fused_computation.640 | loop fusion | flops 27033600 | bytes 4892812 | tf_op jit(solution)/shard_map/add | solution.py:219
  305.1 1.9 collective-permute-start.16
  307.0 5.5 %collective-permute-start.17 = (f32[3,8,1024]{2,0,1:T(4,128)S(1)}, f32[3,8,1024]{2,0,1:T(4,128)}, u32[]{:S(2)}, u32[]{:S(2)}) collective-permute-start(f32[3,8,1024]{2,0,1:T(4,128)S(1)} %get-tuple-element.101), channel_id=1, source_target_pairs={{16,0},{32,16},{48,32},{64,48},{80,64},{96,80},{112,96},{128,112},... | collective-permute-start | bytes 294920 | tf_op jit(solution)/shard_map/ppermute | solution.py:37
  312.6 2.5 collective-permute-start.18
  315.1 1.9 collective-permute-start.19
  317.7 1.9 concatenate.760
  319.6 2.4 collective-permute-done.19
  325.5 22.3 %multiply_add_fusion.11 = f32[4,8,1024]{2,0,1:T(4,128)S(1)} fusion(f32[4,8,1024]{2,0,1:T(4,128)S(1)} %multiply_add_fusion.22, f32[4,8,256]{2,0,1:T(4,128)S(1)} %copy-done.22, f32[4,8,768]{2,0,1:T(4,128)S(1)} %get-tuple-element.149, f32[4,8,512]{2,0,1:T(4,128)S(1)} %copy-done.17, f32[4,8,512]{2,0,1:T(4,128)S(1)} %get-tuple-element.150, ...), kind=kLoop, calls=%fused_computation.443 | loop fusion | flops 27131904 | bytes 5023884 | tf_op jit(solution)/shard_map/add | solution.py:226
  357.4 1.9 collective-permute-start.20
  359.4 5.5 %collective-permute-start.21 = (f32[3,8,1024]{2,0,1:T(4,128)}, f32[3,8,1024]{2,0,1:T(4,128)}, u32[]{:S(2)}, u32[]{:S(2)}) collective-permute-start(f32[3,8,1024]{2,0,1:T(4,128)} %get-tuple-element.49), channel_id=1, source_target_pairs={{16,0},{32,16},{48,32},{64,48},{80,64},{96,80},{112,96},{128,112},... | collective-permute-start | bytes 294920 | tf_op jit(solution)/shard_map/ppermute | solution.py:37
  364.9 3.1 collective-permute-start.22
  368.0 1.9 collective-permute-start.23
  370.7 1.9 concatenate.785
  372.6 2.4 collective-permute-done.23
  378.4 21.8 %multiply_add_fusion = f32[4,8,1024]{2,0,1:T(4,128)S(1)} fusion(f32[4,8,1024]{2,0,1:T(4,128)S(1)} %multiply_add_fusion.11, f32[4,8,256]{2,0,1:T(4,128)S(1)} %get-tuple-element.95, f32[4,8,768]{2,0,1:T(4,128)S(1)} %get-tuple-element.97, f32[4,8,512]{2,0,1:T(4,128)S(1)} %get-tuple-element.99, f32[4,8,512]{2,0,1:T(4,128)S(1)} %get-tuple-element.98, ...), kind=kLoop, calls=%fused_computation.246 | loop fusion | flops 27131904 | bytes 5023884 | tf_op jit(solution)/shard_map/add | solution.py:234
  (758 shorter events, 97.6 us)
Async XLA Ops:
  1.8 16.0 %copy-start = (f32[4,8,1024]{2,1,0:T(8,128)S(1)}, f32[4,8,1024]{2,1,0:T(8,128)}, u32[]{:S(2)}) copy-start(f32[4,8,1024]{2,1,0:T(8,128)} %param.2) | copy-start | bytes 393220
  1.8 39.5 %collective-permute-start = (f32[3,8,1024]{2,0,1:T(4,128)}, f32[3,8,1024]{2,0,1:T(4,128)}, u32[]{:S(2)}, u32[]{:S(2)}) collective-permute-start(f32[3,8,1024]{2,0,1:T(4,128)} %get-tuple-element.352), channel_id=1, source_target_pairs={{0,16},{16,32},{32,48},{48,64},{64,80},{80,96},{96,112},{112,128},... | collective-permute-start | bytes 294920 | tf_op jit(solution)/shard_map/ppermute | solution.py:34
  5.1 36.1 %collective-permute-start.1 = (f32[3,8,1024]{2,0,1:T(4,128)}, f32[3,8,1024]{2,0,1:T(4,128)}, u32[]{:S(2)}, u32[]{:S(2)}) collective-permute-start(f32[3,8,1024]{2,0,1:T(4,128)} %get-tuple-element.353), channel_id=1, source_target_pairs={{16,0},{32,16},{48,32},{64,48},{80,64},{96,80},{112,96},{128,112},... | collective-permute-start | bytes 294920 | tf_op jit(solution)/shard_map/ppermute | solution.py:37
  9.9 30.2 %collective-permute-start.2 = (f32[4,3,1024]{2,0,1:T(4,128)}, f32[4,3,1024]{2,0,1:T(4,128)}, u32[]{:S(2)}, u32[]{:S(2)}) collective-permute-start(f32[4,3,1024]{2,0,1:T(4,128)} %get-tuple-element.350), channel_id=1, source_target_pairs={{0,1},{1,2},{2,3},{3,4},{4,5},{5,6},{6,7},{7,8},{8,9},{9,10},{10,1... | collective-permute-start | bytes 147464 | tf_op jit(solution)/shard_map/ppermute | solution.py:34
  15.8 24.3 %collective-permute-start.3 = (f32[4,3,1024]{2,0,1:T(4,128)}, f32[4,3,1024]{2,0,1:T(4,128)}, u32[]{:S(2)}, u32[]{:S(2)}) collective-permute-start(f32[4,3,1024]{2,0,1:T(4,128)} %get-tuple-element.351), channel_id=1, source_target_pairs={{1,0},{2,1},{3,2},{4,3},{5,4},{6,5},{7,6},{8,7},{9,8},{10,9},{11,1... | collective-permute-start | bytes 147464 | tf_op jit(solution)/shard_map/ppermute | solution.py:37
  106.7 13.8 %collective-permute-start.6 = (f32[4,3,1024]{2,0,1:T(4,128)}, f32[4,3,1024]{2,0,1:T(4,128)}, u32[]{:S(2)}, u32[]{:S(2)}) collective-permute-start(f32[4,3,1024]{2,0,1:T(4,128)} %get-tuple-element.256), channel_id=1, source_target_pairs={{0,1},{1,2},{2,3},{3,4},{4,5},{5,6},{6,7},{7,8},{8,9},{9,10},{10,1... | collective-permute-start | bytes 147464 | tf_op jit(solution)/shard_map/ppermute | solution.py:34
  109.8 10.7 %collective-permute-start.7 = (f32[4,3,1024]{2,0,1:T(4,128)}, f32[4,3,1024]{2,0,1:T(4,128)}, u32[]{:S(2)}, u32[]{:S(2)}) collective-permute-start(f32[4,3,1024]{2,0,1:T(4,128)} %get-tuple-element.257), channel_id=1, source_target_pairs={{1,0},{2,1},{3,2},{4,3},{5,4},{6,5},{7,6},{8,7},{9,8},{10,9},{11,1... | collective-permute-start | bytes 147464 | tf_op jit(solution)/shard_map/ppermute | solution.py:37
  111.7 7.6 %copy-start.10 = (f32[4,14,1024]{2,0,1:T(4,128)}, f32[4,14,1024]{2,0,1:T(4,128)S(1)}, u32[]{:S(2)}) copy-start(f32[4,14,1024]{2,0,1:T(4,128)S(1)} %constant_dynamic-update-slice_fusion.7) | copy-start | bytes 688132
  111.7 9.9 %collective-permute-start.4 = (f32[3,8,1024]{2,0,1:T(4,128)S(1)}, f32[3,8,1024]{2,0,1:T(4,128)}, u32[]{:S(2)}, u32[]{:S(2)}) collective-permute-start(f32[3,8,1024]{2,0,1:T(4,128)S(1)} %get-tuple-element.258), channel_id=1, source_target_pairs={{0,16},{16,32},{32,48},{48,64},{64,80},{80,96},{96,112},{112,128},... | collective-permute-start | bytes 294920 | tf_op jit(solution)/shard_map/ppermute | solution.py:34
  114.5 7.1 %collective-permute-start.5 = (f32[3,8,1024]{2,0,1:T(4,128)S(1)}, f32[3,8,1024]{2,0,1:T(4,128)}, u32[]{:S(2)}, u32[]{:S(2)}) collective-permute-start(f32[3,8,1024]{2,0,1:T(4,128)S(1)} %get-tuple-element.259), channel_id=1, source_target_pairs={{16,0},{32,16},{48,32},{64,48},{80,64},{96,80},{112,96},{128,112},... | collective-permute-start | bytes 294920 | tf_op jit(solution)/shard_map/ppermute | solution.py:37
  158.5 17.6 %collective-permute-start.10 = (f32[4,3,1024]{2,0,1:T(4,128)}, f32[4,3,1024]{2,0,1:T(4,128)}, u32[]{:S(2)}, u32[]{:S(2)}) collective-permute-start(f32[4,3,1024]{2,0,1:T(4,128)} %get-tuple-element.246), channel_id=1, source_target_pairs={{0,1},{1,2},{2,3},{3,4},{4,5},{5,6},{6,7},{7,8},{8,9},{9,10},{10,1... | collective-permute-start | bytes 147464 | tf_op jit(solution)/shard_map/ppermute | solution.py:34
  163.9 12.1 %collective-permute-start.11 = (f32[4,3,1024]{2,0,1:T(4,128)}, f32[4,3,1024]{2,0,1:T(4,128)}, u32[]{:S(2)}, u32[]{:S(2)}) collective-permute-start(f32[4,3,1024]{2,0,1:T(4,128)} %get-tuple-element.247), channel_id=1, source_target_pairs={{1,0},{2,1},{3,2},{4,3},{5,4},{6,5},{7,6},{8,7},{9,8},{10,9},{11,1... | collective-permute-start | bytes 147464 | tf_op jit(solution)/shard_map/ppermute | solution.py:37
  165.9 8.2 %copy-start.11 = (f32[4,14,1024]{2,0,1:T(4,128)}, f32[4,14,1024]{2,0,1:T(4,128)S(1)}, u32[]{:S(2)}) copy-start(f32[4,14,1024]{2,0,1:T(4,128)S(1)} %constant_dynamic-update-slice_fusion.14) | copy-start | bytes 688132
  165.9 11.2 %collective-permute-start.8 = (f32[3,8,1024]{2,0,1:T(4,128)}, f32[3,8,1024]{2,0,1:T(4,128)}, u32[]{:S(2)}, u32[]{:S(2)}) collective-permute-start(f32[3,8,1024]{2,0,1:T(4,128)} %get-tuple-element.248), channel_id=1, source_target_pairs={{0,16},{16,32},{32,48},{48,64},{64,80},{80,96},{96,112},{112,128},... | collective-permute-start | bytes 294920 | tf_op jit(solution)/shard_map/ppermute | solution.py:34
  167.8 9.4 %collective-permute-start.9 = (f32[3,8,1024]{2,0,1:T(4,128)S(1)}, f32[3,8,1024]{2,0,1:T(4,128)}, u32[]{:S(2)}, u32[]{:S(2)}) collective-permute-start(f32[3,8,1024]{2,0,1:T(4,128)S(1)} %get-tuple-element.249), channel_id=1, source_target_pairs={{16,0},{32,16},{48,32},{64,48},{80,64},{96,80},{112,96},{128,112},... | collective-permute-start | bytes 294920 | tf_op jit(solution)/shard_map/ppermute | solution.py:37
  179.1 4.2 %copy-start.16 = (f32[4,8,512]{2,0,1:T(4,128)S(1)}, f32[4,8,512]{2,0,1:T(4,128)}, u32[]{:S(2)}) copy-start(f32[4,8,512]{2,0,1:T(4,128)} %get-tuple-element.245) | copy-start | bytes 196612
  179.1 4.2 %copy-start.19 = (f32[4,8,256]{2,0,1:T(4,128)S(1)}, f32[4,8,256]{2,0,1:T(4,128)}, u32[]{:S(2)}) copy-start(f32[4,8,256]{2,0,1:T(4,128)} %get-tuple-element.240) | copy-start | bytes 98308
  179.1 4.2 %copy-start.20 = (f32[4,8,256]{2,0,1:T(4,128)S(1)}, f32[4,8,256]{2,0,1:T(4,128)}, u32[]{:S(2)}) copy-start(f32[4,8,256]{2,0,1:T(4,128)} %get-tuple-element.241) | copy-start | bytes 98308
  179.1 4.2 %copy-start.66 = (f32[4,8,2]{2,0,1:T(4,128)S(1)}, f32[4,8,2]{2,0,1:T(4,128)}, u32[]{:S(2)}) copy-start(f32[4,8,2]{2,0,1:T(4,128)} %get-tuple-element.205) | copy-start | bytes 772
  179.1 4.2 %copy-start.67 = (f32[4,8,14]{2,0,1:T(4,128)S(1)}, f32[4,8,14]{2,0,1:T(4,128)}, u32[]{:S(2)}) copy-start(f32[4,8,14]{2,0,1:T(4,128)} %get-tuple-element.210) | copy-start | bytes 5380
  179.1 4.2 %copy-start.68 = (f32[4,8,14]{2,0,1:T(4,128)S(1)}, f32[4,8,14]{2,0,1:T(4,128)}, u32[]{:S(2)}) copy-start(f32[4,8,14]{2,0,1:T(4,128)} %get-tuple-element.211) | copy-start | bytes 5380
  179.1 4.2 %copy-start.69 = (f32[4,8,1]{2,0,1:T(4,128)S(1)}, f32[4,8,1]{2,0,1:T(4,128)}, u32[]{:S(2)}) copy-start(f32[4,8,1]{2,0,1:T(4,128)} %get-tuple-element.212) | copy-start | bytes 388
  179.2 4.2 %copy-start.70 = (f32[4,8,1]{2,0,1:T(4,128)S(1)}, f32[4,8,1]{2,0,1:T(4,128)}, u32[]{:S(2)}) copy-start(f32[4,8,1]{2,0,1:T(4,128)} %get-tuple-element.213) | copy-start | bytes 388
  179.2 4.2 %copy-start.71 = (f32[4,8,15]{2,0,1:T(4,128)S(1)}, f32[4,8,15]{2,0,1:T(4,128)}, u32[]{:S(2)}) copy-start(f32[4,8,15]{2,0,1:T(4,128)} %get-tuple-element.218) | copy-start | bytes 5764
  179.2 4.2 %copy-start.72 = (f32[4,8,15]{2,0,1:T(4,128)S(1)}, f32[4,8,15]{2,0,1:T(4,128)}, u32[]{:S(2)}) copy-start(f32[4,8,15]{2,0,1:T(4,128)} %get-tuple-element.219) | copy-start | bytes 5764
  179.2 4.2 %copy-start.73 = (f32[4,8,3]{2,0,1:T(4,128)S(1)}, f32[4,8,3]{2,0,1:T(4,128)}, u32[]{:S(2)}) copy-start(f32[4,8,3]{2,0,1:T(4,128)} %get-tuple-element.220) | copy-start | bytes 1156
  179.2 4.2 %copy-start.74 = (f32[4,8,3]{2,0,1:T(4,128)S(1)}, f32[4,8,3]{2,0,1:T(4,128)}, u32[]{:S(2)}) copy-start(f32[4,8,3]{2,0,1:T(4,128)} %get-tuple-element.221) | copy-start | bytes 1156
  179.2 4.2 %copy-start.75 = (f32[4,8,13]{2,0,1:T(4,128)S(1)}, f32[4,8,13]{2,0,1:T(4,128)}, u32[]{:S(2)}) copy-start(f32[4,8,13]{2,0,1:T(4,128)} %get-tuple-element.226) | copy-start | bytes 4996
  179.2 4.2 %copy-start.76 = (f32[4,8,13]{2,0,1:T(4,128)S(1)}, f32[4,8,13]{2,0,1:T(4,128)}, u32[]{:S(2)}) copy-start(f32[4,8,13]{2,0,1:T(4,128)} %get-tuple-element.227) | copy-start | bytes 4996
  179.2 4.2 %copy-start.77 = (f32[4,8,16]{2,0,1:T(4,128)S(1)}, f32[4,8,16]{2,0,1:T(4,128)}, u32[]{:S(2)}) copy-start(f32[4,8,16]{2,0,1:T(4,128)} %get-tuple-element.228) | copy-start | bytes 6148
  179.2 4.2 %copy-start.78 = (f32[4,8,16]{2,0,1:T(4,128)S(1)}, f32[4,8,16]{2,0,1:T(4,128)}, u32[]{:S(2)}) copy-start(f32[4,8,16]{2,0,1:T(4,128)} %get-tuple-element.229) | copy-start | bytes 6148
  179.2 4.2 %copy-start.79 = (f32[4,8,32]{2,0,1:T(4,128)S(1)}, f32[4,8,32]{2,0,1:T(4,128)}, u32[]{:S(2)}) copy-start(f32[4,8,32]{2,0,1:T(4,128)} %get-tuple-element.232) | copy-start | bytes 12292
  179.3 4.2 %copy-start.80 = (f32[4,8,32]{2,0,1:T(4,128)S(1)}, f32[4,8,32]{2,0,1:T(4,128)}, u32[]{:S(2)}) copy-start(f32[4,8,32]{2,0,1:T(4,128)} %get-tuple-element.233) | copy-start | bytes 12292
  179.3 4.2 %copy-start.81 = (f32[4,8,48]{2,0,1:T(4,128)S(1)}, f32[4,8,48]{2,0,1:T(4,128)}, u32[]{:S(2)}) copy-start(f32[4,8,48]{2,0,1:T(4,128)} %get-tuple-element.236) | copy-start | bytes 18436
  179.3 4.2 %copy-start.82 = (f32[4,8,48]{2,0,1:T(4,128)S(1)}, f32[4,8,48]{2,0,1:T(4,128)}, u32[]{:S(2)}) copy-start(f32[4,8,48]{2,0,1:T(4,128)} %get-tuple-element.237) | copy-start | bytes 18436
  179.3 4.2 %copy-start.163 = (pred[1024]{0:T(1024)(128)(4,1)S(1)}, pred[1024]{0:T(1024)(128)(4,1)}, u32[]{:S(2)}) copy-start(pred[1024]{0:T(1024)(128)(4,1)} %get-tuple-element.370) | copy-start | bytes 3076
  249.7 19.9 %collective-permute-start.12 = (f32[3,8,1024]{2,0,1:T(4,128)}, f32[3,8,1024]{2,0,1:T(4,128)}, u32[]{:S(2)}, u32[]{:S(2)}) collective-permute-start(f32[3,8,1024]{2,0,1:T(4,128)} %get-tuple-element.152), channel_id=1, source_target_pairs={{0,16},{16,32},{32,48},{48,64},{64,80},{80,96},{96,112},{112,128},... | collective-permute-start | bytes 294920 | tf_op jit(solution)/shard_map/ppermute | solution.py:34
  251.6 18.0 %collective-permute-start.13 = (f32[3,8,1024]{2,0,1:T(4,128)}, f32[3,8,1024]{2,0,1:T(4,128)}, u32[]{:S(2)}, u32[]{:S(2)}) collective-permute-start(f32[3,8,1024]{2,0,1:T(4,128)} %get-tuple-element.153), channel_id=1, source_target_pairs={{16,0},{32,16},{48,32},{64,48},{80,64},{96,80},{112,96},{128,112},... | collective-permute-start | bytes 294920 | tf_op jit(solution)/shard_map/ppermute | solution.py:37
  257.2 8.4 %collective-permute-start.14 = (f32[4,3,1024]{2,0,1:T(4,128)}, f32[4,3,1024]{2,0,1:T(4,128)}, u32[]{:S(2)}, u32[]{:S(2)}) collective-permute-start(f32[4,3,1024]{2,0,1:T(4,128)} %get-tuple-element.160), channel_id=1, source_target_pairs={{0,1},{1,2},{2,3},{3,4},{4,5},{5,6},{6,7},{7,8},{8,9},{9,10},{10,1... | collective-permute-start | bytes 147464 | tf_op jit(solution)/shard_map/ppermute | solution.py:34
  261.7 6.9 %collective-permute-start.15 = (f32[4,3,1024]{2,0,1:T(4,128)}, f32[4,3,1024]{2,0,1:T(4,128)}, u32[]{:S(2)}, u32[]{:S(2)}) collective-permute-start(f32[4,3,1024]{2,0,1:T(4,128)} %get-tuple-element.161), channel_id=1, source_target_pairs={{1,0},{2,1},{3,2},{4,3},{5,4},{6,5},{7,6},{8,7},{9,8},{10,9},{11,1... | collective-permute-start | bytes 147464 | tf_op jit(solution)/shard_map/ppermute | solution.py:37
  305.1 18.0 %collective-permute-start.16 = (f32[3,8,1024]{2,0,1:T(4,128)}, f32[3,8,1024]{2,0,1:T(4,128)}, u32[]{:S(2)}, u32[]{:S(2)}) collective-permute-start(f32[3,8,1024]{2,0,1:T(4,128)} %get-tuple-element.100), channel_id=1, source_target_pairs={{0,16},{16,32},{32,48},{48,64},{64,80},{80,96},{96,112},{112,128},... | collective-permute-start | bytes 294920 | tf_op jit(solution)/shard_map/ppermute | solution.py:34
  307.0 16.1 %collective-permute-start.17 = (f32[3,8,1024]{2,0,1:T(4,128)S(1)}, f32[3,8,1024]{2,0,1:T(4,128)}, u32[]{:S(2)}, u32[]{:S(2)}) collective-permute-start(f32[3,8,1024]{2,0,1:T(4,128)S(1)} %get-tuple-element.101), channel_id=1, source_target_pairs={{16,0},{32,16},{48,32},{64,48},{80,64},{96,80},{112,96},{128,112},... | collective-permute-start | bytes 294920 | tf_op jit(solution)/shard_map/ppermute | solution.py:37
  312.6 7.0 %collective-permute-start.18 = (f32[4,3,1024]{2,0,1:T(4,128)}, f32[4,3,1024]{2,0,1:T(4,128)}, u32[]{:S(2)}, u32[]{:S(2)}) collective-permute-start(f32[4,3,1024]{2,0,1:T(4,128)} %get-tuple-element.108), channel_id=1, source_target_pairs={{0,1},{1,2},{2,3},{3,4},{4,5},{5,6},{6,7},{7,8},{8,9},{9,10},{10,1... | collective-permute-start | bytes 147464 | tf_op jit(solution)/shard_map/ppermute | solution.py:34
  315.1 6.9 %collective-permute-start.19 = (f32[4,3,1024]{2,0,1:T(4,128)}, f32[4,3,1024]{2,0,1:T(4,128)}, u32[]{:S(2)}, u32[]{:S(2)}) collective-permute-start(f32[4,3,1024]{2,0,1:T(4,128)} %get-tuple-element.109), channel_id=1, source_target_pairs={{1,0},{2,1},{3,2},{4,3},{5,4},{6,5},{7,6},{8,7},{9,8},{10,9},{11,1... | collective-permute-start | bytes 147464 | tf_op jit(solution)/shard_map/ppermute | solution.py:37
  357.4 18.6 %collective-permute-start.20 = (f32[3,8,1024]{2,0,1:T(4,128)}, f32[3,8,1024]{2,0,1:T(4,128)}, u32[]{:S(2)}, u32[]{:S(2)}) collective-permute-start(f32[3,8,1024]{2,0,1:T(4,128)} %get-tuple-element.48), channel_id=1, source_target_pairs={{0,16},{16,32},{32,48},{48,64},{64,80},{80,96},{96,112},{112,128},... | collective-permute-start | bytes 294920 | tf_op jit(solution)/shard_map/ppermute | solution.py:34
  359.4 16.7 %collective-permute-start.21 = (f32[3,8,1024]{2,0,1:T(4,128)}, f32[3,8,1024]{2,0,1:T(4,128)}, u32[]{:S(2)}, u32[]{:S(2)}) collective-permute-start(f32[3,8,1024]{2,0,1:T(4,128)} %get-tuple-element.49), channel_id=1, source_target_pairs={{16,0},{32,16},{48,32},{64,48},{80,64},{96,80},{112,96},{128,112},... | collective-permute-start | bytes 294920 | tf_op jit(solution)/shard_map/ppermute | solution.py:37
  364.9 7.6 %collective-permute-start.22 = (f32[4,3,1024]{2,0,1:T(4,128)}, f32[4,3,1024]{2,0,1:T(4,128)}, u32[]{:S(2)}, u32[]{:S(2)}) collective-permute-start(f32[4,3,1024]{2,0,1:T(4,128)} %get-tuple-element.56), channel_id=1, source_target_pairs={{0,1},{1,2},{2,3},{3,4},{4,5},{5,6},{6,7},{7,8},{8,9},{9,10},{10,1... | collective-permute-start | bytes 147464 | tf_op jit(solution)/shard_map/ppermute | solution.py:34
  368.0 6.9 %collective-permute-start.23 = (f32[4,3,1024]{2,0,1:T(4,128)}, f32[4,3,1024]{2,0,1:T(4,128)}, u32[]{:S(2)}, u32[]{:S(2)}) collective-permute-start(f32[4,3,1024]{2,0,1:T(4,128)} %get-tuple-element.57), channel_id=1, source_target_pairs={{1,0},{2,1},{3,2},{4,3},{5,4},{6,5},{7,6},{8,7},{9,8},{10,9},{11,1... | collective-permute-start | bytes 147464 | tf_op jit(solution)/shard_map/ppermute | solution.py:37
  (232 other events, 306.9 us)
where the time goes:
time: 404 us; the launch traced here: 401 us
  other arithmetic  144 us (36%)
  starting transfers between devices  81.3 us (20%)
  blocking collectives  79.6 us (20%)
  local copies, waits for them, and re-layouts  77.8 us (19%)
  between operations  9.79 us (2%)
  waiting for transfers between devices  7.92 us (2%)
    pmax x8, blocking collectives, by_axis(): return functools.reduce(lax.pmax, axes, array)  79.6 us
    slice x126, local copies, waits for them, and re-layouts, rolled(): return jnp.roll(grid_values, -offset * stride, axis=-1)  50.3 us
    add x2, other arithmetic, body(): 0.75 * current  44.5 us
    ppermute x12, starting transfers between devices, with_halo(): lax.ppermute(lax.slice_in_dim(block, 0, width, axis=dim), axis, backward)  43.2 us
    ppermute x12, starting transfers between devices, with_halo(): lax.ppermute(lax.slice_in_dim(block, block.shape[dim] - width, None, axis...  38.1 us
    add x2, other arithmetic, body(): current + time_delta * change_rate(slopes, means, disturb_cells, coords,...  31.9 us
    add x2, other arithmetic, body(): current / 3.0  31.4 us
    select_n x12, other arithmetic, border_fix(): return jnp.where(outside, extrapolated, extended)  13.3 us
  transfers between devices with their start and end apart: 24, of which 4 were waited for; matrix products, arithmetic and copies ran while one was open for 9% of the time, Pallas kernels for 0%

commit v1 on v0

v1 whole, which is shorter than its diff:
```python
import functools
import math

import jax
import jax.numpy as jnp
import numpy as np
from jax import lax
from jax.experimental import pallas as pl
from jax.experimental.pallas import tpu as pltpu
from jax.sharding import PartitionSpec as P

HEADINGS = 16
SPEEDS = 16
TURNS = 4
LANES = HEADINGS * SPEEDS * TURNS

NX = 4
NY = 8
SUB = 8
LANE = 128
TILES = LANES // LANE
FX = NX + 6
FY = NY + 6

SCALE = 4.0
step_xy = 0.1
step_heading = 2.0 * math.pi / HEADINGS
accel = 0.5
torque = 0.3
turn_peak = 0.1 * (TURNS - 1) / 2.0
EPS_XY = 0.75e-6 * (SCALE * step_xy) ** 2
EPS_HEADING = 0.75e-6 * (SCALE * step_heading) ** 2
RADIUS = 0.01 * (SCALE * 12.0 * step_xy) ** 2

MESH = pl.DeviceIdType.MESH


def coordinate_tables():
    lanes = np.arange(LANES)
    heading = (-math.pi + ((lanes % HEADINGS) + 0.5) * step_heading).astype(np.float32)
    speed = (1.0 + 0.1 * (lanes // HEADINGS % SPEEDS)).astype(np.float32)
    vx = speed * np.cos(heading)
    vy = speed * np.sin(heading)
    return np.stack([vx, vy]).astype(np.float32).reshape(2, SUB, LANE)


def corrections(s1, s2, s3, x1, x2):
    a = s2 * s3
    b = s1 * s3
    c = s1 * s2
    r1 = a * a
    r2 = b * b
    r3 = c * c
    mid = r1 + r3 + 6.0 * r2
    den_right = mid + (r3 + r3)
    den_left = mid + (r1 + r1)
    y1 = r1 * x1
    y2 = r3 * x2
    both = y1 + y2
    both = both + both
    right = (both + y2) / den_right
    left = (both + y1) / den_left
    return right, left


def smooth_outer(inner, outer_sq, inner_sq, product):
    return (2.5 * inner_sq - 2.75 * product) + outer_sq


def line_slopes(cells, eps):
    n = len(cells) - 6
    diff = [b - a for a, b in zip(cells[:-1], cells[1:])]
    second = [b - a for a, b in zip(diff[:-1], diff[1:])]
    third = [b - a for a, b in zip(second[:-1], second[1:])]
    fourth = [b - a for a, b in zip(third[:-1], third[1:])]
    sq = [e * e for e in second]
    sq_eps = [q + eps for q in sq]
    sq_big = [2.5 * q for q in sq]
    product = [a * b for a, b in zip(second[:-1], second[1:])]
    prod_outer = [2.75 * q for q in product]
    prod_inner = [1.25 * q for q in product]
    rights, lefts = [], []
    for k in range(n + 1):
        s1 = (sq_big[k + 1] - prod_outer[k]) + sq_eps[k]
        s2 = (sq[k + 1] - prod_inner[k + 1]) + sq_eps[k + 2]
        s3 = (sq_big[k + 2] - prod_outer[k + 2]) + sq_eps[k + 3]
        right, left = corrections(s1, s2, s3, fourth[k], fourth[k + 1])
        rights.append(right)
        lefts.append(left)
    sums, gaps = [], []
    for i in range(n):
        right, left = rights[i], lefts[i + 1]
        central = 6.0 * (diff[i + 2] + diff[i + 3]) - (second[i + 3] - second[i + 1])
        sums.append(central + (left - right))
        gaps.append((left + right) - fourth[i + 1])
    return sums, gaps


def edge_correction(g, eps):
    s = g * g + eps
    return (3.0 * eps * eps) * g / (7.0 * (s * s) + 3.0 * eps * eps)


def turn_slopes(cells, eps):
    d0, d1, d2 = (b - a for a, b in zip(cells[:-1], cells[1:]))
    e1 = d1 - d0
    e2 = d2 - d1
    sq1, sq2, p12 = e1 * e1, e2 * e2, e1 * e2
    big1, big2 = 2.5 * sq1, 2.5 * sq2
    one1, one2 = sq1 + eps, sq2 + eps
    x0, x1, x2, x3 = e1, e2 - (e1 + e1), e1 - (e2 + e2), e2
    outer = 2.75 * p12
    right_edge = edge_correction(e1, eps)
    left_edge = edge_correction(e2, eps)
    r0, l0 = corrections(eps, one1, (big1 - outer) + one2, x0, x1)
    r1, l1 = corrections(big1 + eps, (sq1 - 1.25 * p12) + one2, big2 + eps, x1, x2)
    r2, l2 = corrections((big2 - outer) + one1, one2, eps, x2, x3)
    rights, lefts = (right_edge, r0, r1, r2), (l0, l1, l2, left_edge)
    centrals = (
        12.0 * d0 - e1,
        6.0 * (d0 + d1) - e2,
        6.0 * (d1 + d2) + e1,
        12.0 * d2 + e2,
    )
    sums = [c + (le - ri) for c, le, ri in zip(centrals, lefts, rights)]
    gaps = [(le + ri) - x for x, le, ri in zip((x0, x1, x2, x3), lefts, rights)]
    return sums, gaps


def lane_corrections(em, e, ep, epp, eps):
    tm, t, tp = e - em, ep - e, epp - ep
    sq, sqp = e * e, ep * ep
    sqp_eps = sqp + eps
    s1 = e * (2.5 * e - 2.75 * em) + (em * em + eps)
    s2 = e * (e - 1.25 * ep) + sqp_eps
    s3 = ep * (2.5 * ep - 2.75 * epp) + (epp * epp + eps)
    x1 = t - tm
    right, left = corrections(s1, s2, s3, x1, tp - t)
    return right, left, x1


def heading_slopes(f, lane):
    place = lane % HEADINGS

    def moved(v, by):
        near = pltpu.roll(v, (-by) % LANE, 1)
        wrapped = pltpu.roll(v, (HEADINGS - by if by > 0 else -HEADINGS - by) % LANE, 1)
        inside = place < HEADINGS - by if by > 0 else place >= -by
        return jnp.where(inside, near, wrapped)

    d = moved(f, 1) - f
    dm = moved(d, -1)
    e = d - dm
    em, ep, epp = moved(e, -1), moved(e, 1), moved(e, 2)
    right, left, x1 = lane_corrections(em, e, ep, epp, EPS_HEADING)
    right = moved(right, -1)
    return 6.0 * (d + dm) - (ep - em) + (left - right), (left + right) - x1


def speed_slopes(pair, lane):
    first = lane < HEADINGS
    last = lane >= LANE - HEADINGS

    def up(vs):
        r0, r1 = (pltpu.roll(v, LANE - HEADINGS, 1) for v in vs)
        return jnp.where(last, r1, r0), jnp.where(last, r0, r1)

    def down(vs):
        r0, r1 = (pltpu.roll(v, HEADINGS, 1) for v in vs)
        return jnp.where(first, r1, r0), jnp.where(first, r0, r1)

    d = [b - a for a, b in zip(pair, up(pair))]
    dm = list(down(d))
    d[1] = jnp.where(last, dm[1], d[1])
    dm[0] = jnp.where(first, d[0], dm[0])
    e = [a - b for a, b in zip(d, dm)]
    em = down(e)
    ep = up(e)
    epp = list(up(ep))
    epp[1] = jnp.where(last, 0.0, epp[1])
    out = [lane_corrections(em[k], e[k], ep[k], epp[k], EPS_XY) for k in range(2)]
    rights = list(down((out[0][0], out[1][0])))
    rights[0] = jnp.where(first, edge_correction(ep[0], EPS_XY), rights[0])
    sums = [
        6.0 * (d[k] + dm[k]) - (ep[k] - em[k]) + (out[k][1] - rights[k]) for k in range(2)
    ]
    gaps = [(out[k][1] + rights[k]) - out[k][2] for k in range(2)]
    return sums, gaps


def kernel(
    gx_count,
    gy_count,
    u_ref,
    dist_ref,
    coord_ref,
    out_ref,
    frame,
    flat,
    px,
    qx,
    qy,
    ham,
    alpha,
    peak,
    arsend,
    arrecv,
    send_sem,
    recv_sem,
    ar_send_sem,
    ar_recv_sem,
):
    gx = lax.axis_index("gx")
    gy = lax.axis_index("gy")

    barrier = pltpu.get_barrier_semaphore()
    for count, axis in ((gx_count, 0), (gy_count, 1)):

        @pl.loop(1, count)
        def _(k, count=count, axis=axis):
            where = (lax.rem(gx + k, count), gy) if axis == 0 else (gx, lax.rem(gy + k, count))
            pl.semaphore_signal(barrier, inc=1, device_id=where, device_id_type=MESH)

    lane = lax.broadcasted_iota(jnp.int32, (SUB, LANE), 1)

    def cell(s, x, y):
        return (s * FX + x, pl.ds(y * SUB, SUB), slice(None))

    for x in range(NX):
        for j in range(TILES):
            tile = u_ref[x, :, j * LANE : (j + 1) * LANE]
            frame[3 + x, pl.ds(3 * SUB + j, SUB, stride=SUB), :] = SCALE * tile

    def flat_pass(s):
        @pl.loop(0, NX)
        def _(x):
            row = s * FX + 3 + x
            tiles = [frame[row, pl.ds(3 * SUB + j, SUB, stride=SUB), :] for j in range(TILES)]
            parts = [None] * TILES
            for j in range(TILES):
                total, gap = heading_slopes(tiles[j], lane)
                rate = 0.1 * (j // 2 - (TURNS - 1) / 2.0)
                parts[j] = (turn_peak / (12.0 * step_heading)) * gap - (
                    rate / (12.0 * step_heading)
                ) * total
            for c in range(TURNS):
                sums, gaps = speed_slopes(tiles[2 * c : 2 * c + 2], lane)
                for k in range(2):
                    parts[2 * c + k] += (accel / (12.0 * step_xy)) * (gaps[k] - jnp.abs(sums[k]))
            for k in range(2):
                sums, gaps = turn_slopes(tiles[k::2], EPS_XY)
                for c in range(TURNS):
                    parts[2 * c + k] += (torque / (12.0 * step_xy)) * (gaps[c] - jnp.abs(sums[c]))
            for j in range(TILES):
                flat[x, pl.ds(j, SUB, stride=SUB), :] = parts[j]

    def halo(s, way):
        row = s * FX
        if way < 2:
            src = frame.at[pl.ds(row + (4 if way == 0 else 3), 3), pl.ds(3 * SUB, NY * SUB)]
            dst = frame.at[pl.ds(row + (0 if way == 0 else 3 + NX), 3), pl.ds(3 * SUB, NY * SUB)]
            where = (gx + 1, gy) if way == 0 else (gx - 1, gy)
        else:
            src = frame.at[pl.ds(row + 3, NX), pl.ds((NY if way == 2 else 3) * SUB, 3 * SUB)]
            dst = frame.at[
                pl.ds(row + 3, NX), pl.ds((0 if way == 2 else 3 + NY) * SUB, 3 * SUB)
            ]
            where = (gx, gy + 1) if way == 2 else (gx, gy - 1)
        return pltpu.make_async_remote_copy(
            src_ref=src,
            dst_ref=dst,
            send_sem=send_sem.at[s, way],
            recv_sem=recv_sem.at[s, way],
            device_id=where,
            device_id_type=MESH,
        )

    sends = (gx < gx_count - 1, gx > 0, gy < gy_count - 1, gy > 0)
    receives = (gx > 0, gx < gx_count - 1, gy > 0, gy < gy_count - 1)

    def send_halos(s):
        for way in range(4):

            @pl.when(sends[way])
            def _(way=way):
                halo(s, way).start()

    def wait_halos(s):
        for way in range(4):

            @pl.when(receives[way])
            def _(way=way):
                halo(s, way).wait_recv()

            @pl.when(sends[way])
            def _(way=way):
                halo(s, way).wait_send()

    def fill_ghosts(s):
        for low, outside in ((True, gx == 0), (False, gx == gx_count - 1)):

            @pl.when(outside)
            def _(low=low):
                end, inner, step = (3, 4, -1) if low else (2 + NX, 1 + NX, 1)

                @pl.loop(0, NY)
                def _(y):
                    edge = frame[cell(s, end, 3 + y)]
                    slope = edge - frame[cell(s, inner, 3 + y)]
                    for k in (1, 2, 3):
                        frame[cell(s, end + step * k, 3 + y)] = edge + float(k) * slope

        for low, outside in ((True, gy == 0), (False, gy == gy_count - 1)):

            @pl.when(outside)
            def _(low=low):
                end, inner, step = (3, 4, -1) if low else (2 + NY, 1 + NY, 1)

                @pl.loop(0, NX)
                def _(x):
                    edge = frame[cell(s, 3 + x, end)]
                    slope = edge - frame[cell(s, 3 + x, inner)]
                    for k in (1, 2, 3):
                        frame[cell(s, 3 + x, end + step * k)] = edge + float(k) * slope

    def position_pass(s):
        @pl.loop(0, NY)
        def _(y):
            sums, gaps = line_slopes([frame[cell(s, i, 3 + y)] for i in range(FX)], EPS_XY)
            for x in range(NX):
                px[x, pl.ds(y * SUB, SUB), :] = sums[x]
                qx[x, pl.ds(y * SUB, SUB), :] = gaps[x]

        @pl.loop(0, NX)
        def _(x):
            sums, gaps = line_slopes([frame[cell(s, 3 + x, i)] for i in range(FY)], EPS_XY)
            vx = coord_ref[0]
            vy = coord_ref[1]
            top_x, top_y = peak[0], peak[1]
            for y in range(NY):
                at = (x, pl.ds(y * SUB, SUB), slice(None))
                bound = dist_ref[x, y]
                sx, sy = px[at], sums[y]
                square = sx * sx + sy * sy + RADIUS
                inverse = lax.rsqrt(square)
                pull = bound * inverse
                top_x = jnp.maximum(top_x, jnp.abs(vx - pull * sx))
                top_y = jnp.maximum(top_y, jnp.abs(vy - pull * sy))
                ham[at] = flat[at] + (1.0 / (12.0 * step_xy)) * (
                    (pull * square) - (sx * vx + sy * vy)
                )
                qy[at] = gaps[y]
            peak[0] = top_x
            peak[1] = top_y

    half = lane < LANE // 2

    def fold(v):
        for by in (4, 2, 1):
            v = jnp.maximum(v, pltpu.roll(v, by, 0))
        return jnp.maximum(v, pltpu.roll(v, LANE // 2, 1))

    def ar_copy(turn, phase, k):
        count = gy_count if phase == 0 else gx_count
        where = (gx, lax.rem(gy + k, count)) if phase == 0 else (lax.rem(gx + k, count), gy)
        return pltpu.make_async_remote_copy(
            src_ref=arsend.at[2 * turn + phase],
            dst_ref=arrecv.at[2 * turn + phase, k - 1],
            send_sem=ar_send_sem.at[2 * turn + phase],
            recv_sem=ar_recv_sem.at[2 * turn + phase],
            device_id=where,
            device_id_type=MESH,
        )

    def ar_start(turn, phase, row):
        arsend[2 * turn + phase] = row

        @pl.loop(1, gy_count if phase == 0 else gx_count)
        def _(k):
            ar_copy(turn, phase, k).start()

    def ar_finish(turn, phase):
        count = gy_count if phase == 0 else gx_count
        slot = 2 * turn + phase
        every = arrecv.at[slot, pl.ds(0, count - 1)]
        whole = pltpu.make_async_remote_copy(
            src_ref=every,
            dst_ref=every,
            send_sem=ar_send_sem.at[slot],
            recv_sem=ar_recv_sem.at[slot],
            device_id=(gx, gy),
            device_id_type=MESH,
        )
        whole.wait_send()
        whole.wait_recv()
        row = arsend[slot]
        for k in range(count - 1):
            row = jnp.maximum(row, arrecv[slot, k])
        return row

    def own_row():
        return jnp.where(half, fold(peak[0]), fold(peak[1]))[0:1]

    def set_alpha(row):
        row = jnp.broadcast_to(row, (SUB, LANE))
        ax = jnp.max(jnp.where(half, row, 0.0), axis=1, keepdims=True)
        ay = jnp.max(jnp.where(half, 0.0, row), axis=1, keepdims=True)
        ax = jnp.broadcast_to(ax, (SUB, LANE))
        ay = jnp.broadcast_to(ay, (SUB, LANE))
        total = ax / step_xy + ay / step_xy + turn_peak / step_heading
        alpha[0] = (1.0 / (12.0 * step_xy)) * ax
        alpha[1] = (1.0 / (12.0 * step_xy)) * ay
        alpha[2] = 0.75 / (total + accel / step_xy + torque / step_xy)

    peak[...] = jnp.zeros_like(peak)

    @pl.loop(0, 6)
    def _(s):
        part = lax.rem(s, 3)
        flat_pass(s)
        fill_ghosts(s)

        @pl.when(s == 0)
        def _():
            pl.semaphore_wait(barrier, gx_count + gy_count - 2)
            send_halos(s)

        @pl.when(s == 3)
        def _():
            ar_start(1, 1, ar_finish(1, 0))

        wait_halos(s)
        position_pass(s)

        @pl.when(s == 0)
        def _():
            ar_start(0, 0, own_row())
            ar_start(0, 1, ar_finish(0, 0))
            set_alpha(ar_finish(0, 1))
            peak[...] = jnp.zeros_like(peak)

        @pl.when(s == 2)
        def _():
            ar_start(1, 0, own_row())

        @pl.when(s == 3)
        def _():
            set_alpha(ar_finish(1, 1))

        keep = jnp.where(part == 0, 0.0, jnp.where(part == 1, 0.75, 1.0 / 3.0))
        take = jnp.where(part == 0, 1.0, jnp.where(part == 1, 0.25, 2.0 / 3.0))
        base = s - part

        @pl.loop(0, NX)
        def _(x):
            ax, ay, dt = alpha[0], alpha[1], alpha[2]
            for y in range(NY):
                at = (x, pl.ds(y * SUB, SUB), slice(None))
                rate = ham[at] + (ax * qx[at] + ay * qy[at])
                moved = frame[cell(s, 3 + x, 3 + y)] + dt * rate
                frame[cell(s + 1, 3 + x, 3 + y)] = (
                    keep * frame[cell(base, 3 + x, 3 + y)] + take * moved
                )

        @pl.when(s < 5)
        def _():
            send_halos(s + 1)

    for x in range(NX):
        for j in range(TILES):
            tile = frame[6 * FX + 3 + x, pl.ds(3 * SUB + j, SUB, stride=SUB), :]
            out_ref[x, :, j * LANE : (j + 1) * LANE] = (1.0 / SCALE) * tile


def body(gx_count, gy_count, initial_value, disturbance):
    most = max(gx_count, gy_count)
    return pl.pallas_call(
        functools.partial(kernel, gx_count, gy_count),
        out_shape=jax.ShapeDtypeStruct((NX, NY, LANES), jnp.float32),
        in_specs=[
            pl.BlockSpec(memory_space=pltpu.VMEM),
            pl.BlockSpec(memory_space=pltpu.SMEM),
            pl.BlockSpec(memory_space=pltpu.VMEM),
        ],
        out_specs=pl.BlockSpec(memory_space=pltpu.VMEM),
        scratch_shapes=[
            pltpu.VMEM((7 * FX, FY * SUB, LANE), jnp.float32),
            pltpu.VMEM((NX, NY * SUB, LANE), jnp.float32),
            pltpu.VMEM((NX, NY * SUB, LANE), jnp.float32),
            pltpu.VMEM((NX, NY * SUB, LANE), jnp.float32),
            pltpu.VMEM((NX, NY * SUB, LANE), jnp.float32),
            pltpu.VMEM((NX, NY * SUB, LANE), jnp.float32),
            pltpu.VMEM((3, SUB, LANE), jnp.float32),
            pltpu.VMEM((2, SUB, LANE), jnp.float32),
            pltpu.VMEM((4, 1, LANE), jnp.float32),
            pltpu.VMEM((4, most - 1, 1, LANE), jnp.float32),
            pltpu.SemaphoreType.DMA((6, 4)),
            pltpu.SemaphoreType.DMA((6, 4)),
            pltpu.SemaphoreType.DMA((4,)),
            pltpu.SemaphoreType.DMA((4,)),
        ],
        compiler_params=pltpu.CompilerParams(collective_id=0, has_side_effects=True),
    )(initial_value, disturbance, jnp.asarray(coordinate_tables()))


def solution(mesh):
    placed = (P("gx", "gy", None), P("gx", "gy"))
    return jax.shard_map(
        functools.partial(body, mesh.shape["gx"], mesh.shape["gy"]),
        mesh=mesh,
        in_specs=placed,
        out_specs=P("gx", "gy", None),
        check_vma=False,
    )
```

time: 404 us -> 59.2 us (0.15)
  the two profiles are of different devices: /device:TPU:99 before, /device:TPU:1 now
where the time goes in v1:
time: 59.2 us; the launch traced here: 58.1 us
  Pallas kernels  56.5 us (95%)
  local copies, waits for them, and re-layouts  1.57 us (3%)
    pallas_call x1, Pallas kernels, body(): pl.pallas_call(functools.partial(kernel, gx_count, gy_count), out_shape=j...  56.5 us
    unnamed x1, local copies, waits for them, and re-layouts  1.57 us

profile of v1, /device:TPU:1, one launch (start us, length us, event | category | flops | bytes accessed | tf_op | source)
XLA Modules:
  0.0 58.1 jit_solution(9558961992148854935)
XLA Ops:
  0.0 56.5 %shard_map.37 = f32[4,8,1024]{2,1,0:T(8,128)} custom-call(f32[4,8,1024]{2,1,0:T(8,128)} %u_ref.1, f32[4,8]{1,0:T(4,128)} %dist_ref.1, f32[2,8,128]{2,1,0:T(8,128)} %constant.2.clone.coord_ref), custom_call_target="tpu_custom_call" | custom-call | tf_op jit(solution)/shard_map/pallas_call | solution.py:477
  56.5 1.6 %copy.5 = f32[4,8,1024]{2,1,0:T(8,128)} copy(f32[4,8,1024]{2,1,0:T(8,128)} %shard_map.37) | data formatting | bytes 262144

commit v2 on v1

--- a/solution.py
+++ b/solution.py
@@ -191,13 +191,16 @@
 def kernel(
     gx_count,
     gy_count,
+    u_hbm,
+    dist_hbm,
+    coord_hbm,
+    out_ref,
     u_ref,
     dist_ref,
     coord_ref,
-    out_ref,
     frame,
     flat,
-    px,
+    py,
     qx,
     qy,
     ham,
@@ -205,14 +208,26 @@
     peak,
     arsend,
     arrecv,
-    send_sem,
-    recv_sem,
+    load_sem,
+    send_x_sem,
+    recv_x_sem,
+    send_y_sem,
+    recv_y_sem,
     ar_send_sem,
     ar_recv_sem,
 ):
     gx = lax.axis_index("gx")
     gy = lax.axis_index("gy")
 
+    loads = [
+        pltpu.make_async_copy(src, dst, load_sem.at[k])
+        for k, (src, dst) in enumerate(
+            ((u_hbm, u_ref), (dist_hbm, dist_ref), (coord_hbm, coord_ref))
+        )
+    ]
+    for load in loads:
+        load.start()
+
     barrier = pltpu.get_barrier_semaphore()
     for count, axis in ((gx_count, 0), (gy_count, 1)):
 
@@ -225,6 +240,9 @@
 
     def cell(s, x, y):
         return (s * FX + x, pl.ds(y * SUB, SUB), slice(None))
+
+    for load in loads:
+        load.wait()
 
     for x in range(NX):
         for j in range(TILES):
@@ -254,47 +272,65 @@
             for j in range(TILES):
                 flat[x, pl.ds(j, SUB, stride=SUB), :] = parts[j]
 
-    def halo(s, way):
+    sends = (gx < gx_count - 1, gx > 0, gy < gy_count - 1, gy > 0)
+    receives = (gx > 0, gx < gx_count - 1, gy > 0, gy < gy_count - 1)
+
+    def halo_x(s, way, y):
         row = s * FX
-        if way < 2:
-            src = frame.at[pl.ds(row + (4 if way == 0 else 3), 3), pl.ds(3 * SUB, NY * SUB)]
-            dst = frame.at[pl.ds(row + (0 if way == 0 else 3 + NX), 3), pl.ds(3 * SUB, NY * SUB)]
-            where = (gx + 1, gy) if way == 0 else (gx - 1, gy)
-        else:
-            src = frame.at[pl.ds(row + 3, NX), pl.ds((NY if way == 2 else 3) * SUB, 3 * SUB)]
-            dst = frame.at[
-                pl.ds(row + 3, NX), pl.ds((0 if way == 2 else 3 + NY) * SUB, 3 * SUB)
-            ]
-            where = (gx, gy + 1) if way == 2 else (gx, gy - 1)
+        turn = lax.rem(s, 2)
+        at = pl.ds((3 + y) * SUB, SUB)
         return pltpu.make_async_remote_copy(
-            src_ref=src,
-            dst_ref=dst,
-            send_sem=send_sem.at[s, way],
-            recv_sem=recv_sem.at[s, way],
-            device_id=where,
+            src_ref=frame.at[pl.ds(row + (4 if way == 0 else 3), 3), at],
+            dst_ref=frame.at[pl.ds(row + (0 if way == 0 else 3 + NX), 3), at],
+            send_sem=send_x_sem.at[turn, way, y],
+            recv_sem=recv_x_sem.at[turn, way, y],
+            device_id=(gx + 1, gy) if way == 0 else (gx - 1, gy),
             device_id_type=MESH,
         )
 
-    sends = (gx < gx_count - 1, gx > 0, gy < gy_count - 1, gy > 0)
-    receives = (gx > 0, gx < gx_count - 1, gy > 0, gy < gy_count - 1)
-
-    def send_halos(s):
-        for way in range(4):
+    def halo_y(s, way):
+        rows = pl.ds(s * FX + 3, NX)
+        turn = lax.rem(s, 2)
+        return pltpu.make_async_remote_copy(
+            src_ref=frame.at[rows, pl.ds((NY if way == 0 else 3) * SUB, 3 * SUB)],
+            dst_ref=frame.at[rows, pl.ds((0 if way == 0 else 3 + NY) * SUB, 3 * SUB)],
+            send_sem=send_y_sem.at[turn, way],
+            recv_sem=recv_y_sem.at[turn, way],
+            device_id=(gx, gy + 1) if way == 0 else (gx, gy - 1),
+            device_id_type=MESH,
+        )
+
+    def column(i):
+        return jnp.where(i < 3, i, jnp.where(i < 6, i + 2, i - 3))
+
+    def send_column(s, y):
+        for way in range(2):
 
             @pl.when(sends[way])
             def _(way=way):
-                halo(s, way).start()
-
-    def wait_halos(s):
-        for way in range(4):
-
-            @pl.when(receives[way])
-            def _(way=way):
-                halo(s, way).wait_recv()
+                halo_x(s, way, y).start()
+
+    def send_rows(s, i):
+        @pl.when(jnp.logical_and(i == 2, sends[3]))
+        def _():
+            halo_y(s, 1).start()
+
+        @pl.when(jnp.logical_and(i == 5, sends[2]))
+        def _():
+            halo_y(s, 0).start()
+
+    def finish_sends(s):
+        for way in range(2):
 
             @pl.when(sends[way])
             def _(way=way):
-                halo(s, way).wait_send()
+                @pl.loop(0, NY)
+                def _(y):
+                    halo_x(s, way, y).wait_send()
+
+            @pl.when(sends[2 + way])
+            def _(way=way):
+                halo_y(s, way).wait_send()
 
     def fill_ghosts(s):
         for low, outside in ((True, gx == 0), (False, gx == gx_count - 1)):
@@ -323,35 +359,46 @@
                     for k in (1, 2, 3):
                         frame[cell(s, 3 + x, end + step * k)] = edge + float(k) * slope
 
-    def position_pass(s):
-        @pl.loop(0, NY)
-        def _(y):
-            sums, gaps = line_slopes([frame[cell(s, i, 3 + y)] for i in range(FX)], EPS_XY)
-            for x in range(NX):
-                px[x, pl.ds(y * SUB, SUB), :] = sums[x]
-                qx[x, pl.ds(y * SUB, SUB), :] = gaps[x]
+    def second_pass(s):
+        for way in range(2):
+
+            @pl.when(receives[2 + way])
+            def _(way=way):
+                halo_y(s, way).wait_recv()
 
         @pl.loop(0, NX)
         def _(x):
             sums, gaps = line_slopes([frame[cell(s, 3 + x, i)] for i in range(FY)], EPS_XY)
-            vx = coord_ref[0]
-            vy = coord_ref[1]
-            top_x, top_y = peak[0], peak[1]
             for y in range(NY):
-                at = (x, pl.ds(y * SUB, SUB), slice(None))
-                bound = dist_ref[x, y]
-                sx, sy = px[at], sums[y]
-                square = sx * sx + sy * sy + RADIUS
-                inverse = lax.rsqrt(square)
-                pull = bound * inverse
-                top_x = jnp.maximum(top_x, jnp.abs(vx - pull * sx))
-                top_y = jnp.maximum(top_y, jnp.abs(vy - pull * sy))
-                ham[at] = flat[at] + (1.0 / (12.0 * step_xy)) * (
-                    (pull * square) - (sx * vx + sy * vy)
-                )
-                qy[at] = gaps[y]
-            peak[0] = top_x
-            peak[1] = top_y
+                py[x, pl.ds(y * SUB, SUB), :] = sums[y]
+                qy[x, pl.ds(y * SUB, SUB), :] = gaps[y]
+
+    def first_slopes(s, y):
+        for way in range(2):
+
+            @pl.when(receives[way])
+            def _(way=way):
+                halo_x(s, way, y).wait_recv()
+
+        sums, gaps = line_slopes([frame[cell(s, i, 3 + y)] for i in range(FX)], EPS_XY)
+        vx = coord_ref[0]
+        vy = coord_ref[1]
+        top_x, top_y = peak[0], peak[1]
+        rates = []
+        for x in range(NX):
+            at = (x, pl.ds(y * SUB, SUB), slice(None))
+            bound = dist_ref[x, y]
+            sx, sy = sums[x], py[at]
+            square = sx * sx + sy * sy + RADIUS
+            pull = bound * lax.rsqrt(square)
+            top_x = jnp.maximum(top_x, jnp.abs(vx - pull * sx))
+            top_y = jnp.maximum(top_y, jnp.abs(vy - pull * sy))
+            rates.append(
+                flat[at] + (1.0 / (12.0 * step_xy)) * ((pull * square) - (sx * vx + sy * vy))
+            )
+        peak[0] = top_x
+        peak[1] = top_y
+        return rates, gaps
 
     half = lane < LANE // 2
 
@@ -417,54 +464,85 @@
     @pl.loop(0, 6)
     def _(s):
         part = lax.rem(s, 3)
+        base = s - part
+        keep = jnp.where(part == 0, 0.0, jnp.where(part == 1, 0.75, 1.0 / 3.0))
+        take = jnp.where(part == 0, 1.0, jnp.where(part == 1, 0.25, 2.0 / 3.0))
+
         flat_pass(s)
         fill_ghosts(s)
 
         @pl.when(s == 0)
         def _():
             pl.semaphore_wait(barrier, gx_count + gy_count - 2)
-            send_halos(s)
+
+            @pl.loop(0, NY)
+            def _(i):
+                send_column(s, column(i))
+                send_rows(s, i)
+
+        second_pass(s)
 
         @pl.when(s == 3)
         def _():
             ar_start(1, 1, ar_finish(1, 0))
 
-        wait_halos(s)
-        position_pass(s)
-
-        @pl.when(s == 0)
-        def _():
-            ar_start(0, 0, own_row())
-            ar_start(0, 1, ar_finish(0, 0))
-            set_alpha(ar_finish(0, 1))
-            peak[...] = jnp.zeros_like(peak)
-
-        @pl.when(s == 2)
-        def _():
-            ar_start(1, 0, own_row())
-
-        @pl.when(s == 3)
-        def _():
-            set_alpha(ar_finish(1, 1))
-
-        keep = jnp.where(part == 0, 0.0, jnp.where(part == 1, 0.75, 1.0 / 3.0))
-        take = jnp.where(part == 0, 1.0, jnp.where(part == 1, 0.25, 2.0 / 3.0))
-        base = s - part
-
-        @pl.loop(0, NX)
-        def _(x):
+        def advance(y, rates, gaps):
             ax, ay, dt = alpha[0], alpha[1], alpha[2]
-            for y in range(NY):
+            for x in range(NX):
                 at = (x, pl.ds(y * SUB, SUB), slice(None))
-                rate = ham[at] + (ax * qx[at] + ay * qy[at])
+                rate = rates[x] + (ax * gaps[x] + ay * qy[at])
                 moved = frame[cell(s, 3 + x, 3 + y)] + dt * rate
                 frame[cell(s + 1, 3 + x, 3 + y)] = (
                     keep * frame[cell(base, 3 + x, 3 + y)] + take * moved
                 )
 
-        @pl.when(s < 5)
-        def _():
-            send_halos(s + 1)
+        def send_next(i, y):
+            @pl.when(s < 5)
+            def _():
+                send_column(s + 1, y)
+                send_rows(s + 1, i)
+
+        @pl.when(part > 0)
+        def _():
+            @pl.loop(0, NY)
+            def _(i):
+                y = column(i)
+                advance(y, *first_slopes(s, y))
+                send_next(i, y)
+
+        @pl.when(part == 0)
+        def _():
+            @pl.loop(0, NY)
+            def _(y):
+                rates, gaps = first_slopes(s, y)
+                for x in range(NX):
+                    at = (x, pl.ds(y * SUB, SUB), slice(None))
+                    ham[at] = rates[x]
+                    qx[at] = gaps[x]
+
+            @pl.when(s == 0)
+            def _():
+                ar_start(0, 0, own_row())
+                ar_start(0, 1, ar_finish(0, 0))
+                set_alpha(ar_finish(0, 1))
+                peak[...] = jnp.zeros_like(peak)
+
+            @pl.when(s == 3)
+            def _():
+                set_alpha(ar_finish(1, 1))
+
+            @pl.loop(0, NY)
+            def _(i):
+                y = column(i)
+                at = [(x, pl.ds(y * SUB, SUB), slice(None)) for x in range(NX)]
+                advance(y, [ham[a] for a in at], [qx[a] for a in at])
+                send_next(i, y)
+
+        @pl.when(s == 2)
+        def _():
+            ar_start(1, 0, own_row())
+
+        finish_sends(s)
 
     for x in range(NX):
         for j in range(TILES):
@@ -477,13 +555,12 @@
     return pl.pallas_call(
         functools.partial(kernel, gx_count, gy_count),
         out_shape=jax.ShapeDtypeStruct((NX, NY, LANES), jnp.float32),
-        in_specs=[
-            pl.BlockSpec(memory_space=pltpu.VMEM),
-            pl.BlockSpec(memory_space=pltpu.SMEM),
-            pl.BlockSpec(memory_space=pltpu.VMEM),
-        ],
+        in_specs=[pl.BlockSpec(memory_space=pl.ANY)] * 3,
         out_specs=pl.BlockSpec(memory_space=pltpu.VMEM),
         scratch_shapes=[
+            pltpu.VMEM((NX, NY, LANES), jnp.float32),
+            pltpu.SMEM((NX, NY), jnp.float32),
+            pltpu.VMEM((2, SUB, LANE), jnp.float32),
             pltpu.VMEM((7 * FX, FY * SUB, LANE), jnp.float32),
             pltpu.VMEM((NX, NY * SUB, LANE), jnp.float32),
             pltpu.VMEM((NX, NY * SUB, LANE), jnp.float32),
@@ -494,8 +571,11 @@
             pltpu.VMEM((2, SUB, LANE), jnp.float32),
             pltpu.VMEM((4, 1, LANE), jnp.float32),
             pltpu.VMEM((4, most - 1, 1, LANE), jnp.float32),
-            pltpu.SemaphoreType.DMA((6, 4)),
-            pltpu.SemaphoreType.DMA((6, 4)),
+            pltpu.SemaphoreType.DMA((3,)),
+            pltpu.SemaphoreType.DMA((2, 2, NY)),
+            pltpu.SemaphoreType.DMA((2, 2, NY)),
+            pltpu.SemaphoreType.DMA((2, 2)),
+            pltpu.SemaphoreType.DMA((2, 2)),
             pltpu.SemaphoreType.DMA((4,)),
             pltpu.SemaphoreType.DMA((4,)),
         ],

time: 59.2 us -> 54 us (0.912)
  Pallas kernels: 56.5 us -> 51.9 us
    pallas_call x1, Pallas kernels: 56.5 us -> 51.9 us  [body(): pl.pallas_call(functools.partial(kernel, gx_count, gy_count), out_shape=j...]
where the time goes in v2:
time: 54 us; the launch traced here: 53.4 us
  Pallas kernels  51.9 us (96%)
  local copies, waits for them, and re-layouts  1.57 us (3%)
    pallas_call x1, Pallas kernels, body(): pl.pallas_call(functools.partial(kernel, gx_count, gy_count), out_shape=j...  51.9 us
    unnamed x1, local copies, waits for them, and re-layouts  1.57 us

profile of v2, /device:TPU:1, one launch (start us, length us, event | category | flops | bytes accessed | tf_op | source)
XLA Modules:
  0.0 53.4 jit_solution(5444374784166349024)
XLA Ops:
  0.0 51.9 %shard_map.37 = f32[4,8,1024]{2,1,0:T(8,128)} custom-call(f32[4,8,1024]{2,1,0:T(8,128)} %u_hbm.1, f32[4,8]{1,0:T(4,128)} %dist_hbm.1, f32[2,8,128]{2,1,0:T(8,128)} %constant.2.clone.coord_hbm), custom_call_target="tpu_custom_call" | custom-call | tf_op jit(solution)/shard_map/pallas_call | solution.py:555
  51.9 1.6 %copy.5 = f32[4,8,1024]{2,1,0:T(8,128)} copy(f32[4,8,1024]{2,1,0:T(8,128)} %shard_map.37) | data formatting | bytes 262144

commit v3 on v2

--- a/solution.py
+++ b/solution.py
@@ -201,9 +201,7 @@
     frame,
     flat,
     py,
-    qx,
-    qy,
-    ham,
+    rates,
     alpha,
     peak,
     arsend,
@@ -213,6 +211,9 @@
     recv_x_sem,
     send_y_sem,
     recv_y_sem,
+    rate_send_sem,
+    rate_recv_sem,
+    rate_recv_x_sem,
     ar_send_sem,
     ar_recv_sem,
 ):
@@ -231,8 +232,9 @@
     barrier = pltpu.get_barrier_semaphore()
     for count, axis in ((gx_count, 0), (gy_count, 1)):
 
-        @pl.loop(1, count)
-        def _(k, count=count, axis=axis):
+        @pl.loop(0, count - 1)
+        def _(i, count=count, axis=axis):
+            k = lax.rem(i + count // 3, count - 1) + 1
             where = (lax.rem(gx + k, count), gy) if axis == 0 else (gx, lax.rem(gy + k, count))
             pl.semaphore_signal(barrier, inc=1, device_id=where, device_id_type=MESH)
 
@@ -282,7 +284,7 @@
         return pltpu.make_async_remote_copy(
             src_ref=frame.at[pl.ds(row + (4 if way == 0 else 3), 3), at],
             dst_ref=frame.at[pl.ds(row + (0 if way == 0 else 3 + NX), 3), at],
-            send_sem=send_x_sem.at[turn, way, y],
+            send_sem=send_x_sem.at[turn, way],
             recv_sem=recv_x_sem.at[turn, way, y],
             device_id=(gx + 1, gy) if way == 0 else (gx - 1, gy),
             device_id_type=MESH,
@@ -320,17 +322,85 @@
             halo_y(s, 0).start()
 
     def finish_sends(s):
+        turn = lax.rem(s, 2)
+        every = frame.at[pl.ds(0, 3), pl.ds(3 * SUB, NY * SUB)]
         for way in range(2):
 
             @pl.when(sends[way])
             def _(way=way):
-                @pl.loop(0, NY)
-                def _(y):
-                    halo_x(s, way, y).wait_send()
+                pltpu.make_async_remote_copy(
+                    src_ref=every,
+                    dst_ref=every,
+                    send_sem=send_x_sem.at[turn, way],
+                    recv_sem=recv_x_sem.at[turn, way, 0],
+                    device_id=(gx, gy),
+                    device_id_type=MESH,
+                ).wait_send()
 
             @pl.when(sends[2 + way])
             def _(way=way):
                 halo_y(s, way).wait_send()
+
+    def rate_x(way, y):
+        at = pl.ds((3 + y) * SUB, SUB)
+        return pltpu.make_async_remote_copy(
+            src_ref=rates.at[pl.ds(0, 3), pl.ds(4 if way == 0 else 3, 3), at],
+            dst_ref=rates.at[pl.ds(0, 3), pl.ds(0 if way == 0 else 3 + NX, 3), at],
+            send_sem=rate_send_sem.at[way],
+            recv_sem=rate_recv_x_sem.at[way, y],
+            device_id=(gx + 1, gy) if way == 0 else (gx - 1, gy),
+            device_id_type=MESH,
+        )
+
+    def rate_y(way):
+        rows = pl.ds(3, NX)
+        return pltpu.make_async_remote_copy(
+            src_ref=rates.at[pl.ds(0, 3), rows, pl.ds((NY if way == 0 else 3) * SUB, 3 * SUB)],
+            dst_ref=rates.at[pl.ds(0, 3), rows, pl.ds((0 if way == 0 else 3 + NY) * SUB, 3 * SUB)],
+            send_sem=rate_send_sem.at[2 + way],
+            recv_sem=rate_recv_sem.at[way],
+            device_id=(gx, gy + 1) if way == 0 else (gx, gy - 1),
+            device_id_type=MESH,
+        )
+
+    def send_rates(i, y):
+        for way in range(2):
+
+            @pl.when(sends[way])
+            def _(way=way):
+                rate_x(way, y).start()
+
+        @pl.when(jnp.logical_and(i == 2, sends[3]))
+        def _():
+            rate_y(1).start()
+
+        @pl.when(jnp.logical_and(i == 5, sends[2]))
+        def _():
+            rate_y(0).start()
+
+    def finish_rates():
+        every = rates.at[pl.ds(0, 3), pl.ds(0, 3), pl.ds(3 * SUB, NY * SUB)]
+        for way in range(2):
+
+            @pl.when(sends[way])
+            def _(way=way):
+                pltpu.make_async_remote_copy(
+                    src_ref=every,
+                    dst_ref=every,
+                    send_sem=rate_send_sem.at[way],
+                    recv_sem=rate_recv_x_sem.at[way, 0],
+                    device_id=(gx, gy),
+                    device_id_type=MESH,
+                ).wait_send()
+
+            @pl.when(sends[2 + way])
+            def _(way=way):
+                rate_y(way).wait_send()
+
+    def first_move(s, x, y):
+        at = pl.ds(y * SUB, SUB)
+        rate = rates[0, x, at, :] + (alpha[0] * rates[1, x, at, :] + alpha[1] * rates[2, x, at, :])
+        frame[cell(s, x, y)] = frame[cell(s - 1, x, y)] + alpha[2] * rate
 
     def fill_ghosts(s):
         for low, outside in ((True, gx == 0), (False, gx == gx_count - 1)):
@@ -359,32 +429,37 @@
                     for k in (1, 2, 3):
                         frame[cell(s, 3 + x, end + step * k)] = edge + float(k) * slope
 
-    def second_pass(s):
+    def second_pass(s, part):
+        slot = jnp.where(part == 0, 2, 3)
+
         for way in range(2):
 
-            @pl.when(receives[2 + way])
+            @pl.when(jnp.logical_and(receives[2 + way], part != 1))
             def _(way=way):
                 halo_y(s, way).wait_recv()
+
+            @pl.when(jnp.logical_and(receives[2 + way], part == 1))
+            def _(way=way):
+                rate_y(way).wait_recv()
+
+                @pl.loop(0, NX)
+                def _(x):
+                    for k in range(3):
+                        first_move(s, 3 + x, k + (0 if way == 0 else 3 + NY))
 
         @pl.loop(0, NX)
         def _(x):
             sums, gaps = line_slopes([frame[cell(s, 3 + x, i)] for i in range(FY)], EPS_XY)
             for y in range(NY):
                 py[x, pl.ds(y * SUB, SUB), :] = sums[y]
-                qy[x, pl.ds(y * SUB, SUB), :] = gaps[y]
+                rates[slot, 3 + x, pl.ds((3 + y) * SUB, SUB), :] = gaps[y]
 
     def first_slopes(s, y):
-        for way in range(2):
-
-            @pl.when(receives[way])
-            def _(way=way):
-                halo_x(s, way, y).wait_recv()
-
         sums, gaps = line_slopes([frame[cell(s, i, 3 + y)] for i in range(FX)], EPS_XY)
         vx = coord_ref[0]
         vy = coord_ref[1]
         top_x, top_y = peak[0], peak[1]
-        rates = []
+        moves = []
         for x in range(NX):
             at = (x, pl.ds(y * SUB, SUB), slice(None))
             bound = dist_ref[x, y]
@@ -393,12 +468,12 @@
             pull = bound * lax.rsqrt(square)
             top_x = jnp.maximum(top_x, jnp.abs(vx - pull * sx))
             top_y = jnp.maximum(top_y, jnp.abs(vy - pull * sy))
-            rates.append(
+            moves.append(
                 flat[at] + (1.0 / (12.0 * step_xy)) * ((pull * square) - (sx * vx + sy * vy))
             )
         peak[0] = top_x
         peak[1] = top_y
-        return rates, gaps
+        return moves, gaps
 
     half = lane < LANE // 2
 
@@ -422,9 +497,11 @@
     def ar_start(turn, phase, row):
         arsend[2 * turn + phase] = row
 
-        @pl.loop(1, gy_count if phase == 0 else gx_count)
-        def _(k):
-            ar_copy(turn, phase, k).start()
+        count = gy_count if phase == 0 else gx_count
+
+        @pl.loop(0, count - 1)
+        def _(i):
+            ar_copy(turn, phase, lax.rem(i + count // 3, count - 1) + 1).start()
 
     def ar_finish(turn, phase):
         count = gy_count if phase == 0 else gx_count
@@ -461,64 +538,42 @@
 
     peak[...] = jnp.zeros_like(peak)
 
+    pl.semaphore_wait(barrier, gx_count + gy_count - 2)
+
+    @pl.loop(0, NY)
+    def _(i):
+        send_column(0, column(i))
+        send_rows(0, i)
+
     @pl.loop(0, 6)
     def _(s):
         part = lax.rem(s, 3)
         base = s - part
-        keep = jnp.where(part == 0, 0.0, jnp.where(part == 1, 0.75, 1.0 / 3.0))
-        take = jnp.where(part == 0, 1.0, jnp.where(part == 1, 0.25, 2.0 / 3.0))
 
         flat_pass(s)
         fill_ghosts(s)
-
-        @pl.when(s == 0)
-        def _():
-            pl.semaphore_wait(barrier, gx_count + gy_count - 2)
-
-            @pl.loop(0, NY)
-            def _(i):
-                send_column(s, column(i))
-                send_rows(s, i)
-
-        second_pass(s)
+        second_pass(s, part)
 
         @pl.when(s == 3)
         def _():
             ar_start(1, 1, ar_finish(1, 0))
 
-        def advance(y, rates, gaps):
-            ax, ay, dt = alpha[0], alpha[1], alpha[2]
-            for x in range(NX):
-                at = (x, pl.ds(y * SUB, SUB), slice(None))
-                rate = rates[x] + (ax * gaps[x] + ay * qy[at])
-                moved = frame[cell(s, 3 + x, 3 + y)] + dt * rate
-                frame[cell(s + 1, 3 + x, 3 + y)] = (
-                    keep * frame[cell(base, 3 + x, 3 + y)] + take * moved
-                )
-
-        def send_next(i, y):
-            @pl.when(s < 5)
-            def _():
-                send_column(s + 1, y)
-                send_rows(s + 1, i)
-
-        @pl.when(part > 0)
+        @pl.when(part == 0)
         def _():
             @pl.loop(0, NY)
             def _(i):
                 y = column(i)
-                advance(y, *first_slopes(s, y))
-                send_next(i, y)
-
-        @pl.when(part == 0)
-        def _():
-            @pl.loop(0, NY)
-            def _(y):
-                rates, gaps = first_slopes(s, y)
+                for way in range(2):
+
+                    @pl.when(receives[way])
+                    def _(way=way):
+                        halo_x(s, way, y).wait_recv()
+
+                moves, gaps = first_slopes(s, y)
                 for x in range(NX):
-                    at = (x, pl.ds(y * SUB, SUB), slice(None))
-                    ham[at] = rates[x]
-                    qx[at] = gaps[x]
+                    rates[0, 3 + x, pl.ds((3 + y) * SUB, SUB), :] = moves[x]
+                    rates[1, 3 + x, pl.ds((3 + y) * SUB, SUB), :] = gaps[x]
+                send_rates(i, y)
 
             @pl.when(s == 0)
             def _():
@@ -532,17 +587,58 @@
                 set_alpha(ar_finish(1, 1))
 
             @pl.loop(0, NY)
+            def _(y):
+                for x in range(NX):
+                    first_move(s + 1, 3 + x, 3 + y)
+
+            finish_sends(s)
+
+        @pl.when(part > 0)
+        def _():
+            keep = jnp.where(part == 1, 0.75, 1.0 / 3.0)
+            take = jnp.where(part == 1, 0.25, 2.0 / 3.0)
+
+            @pl.loop(0, NY)
             def _(i):
                 y = column(i)
-                at = [(x, pl.ds(y * SUB, SUB), slice(None)) for x in range(NX)]
-                advance(y, [ham[a] for a in at], [qx[a] for a in at])
-                send_next(i, y)
+                for way in range(2):
+
+                    @pl.when(jnp.logical_and(receives[way], part == 2))
+                    def _(way=way):
+                        halo_x(s, way, y).wait_recv()
+
+                    @pl.when(jnp.logical_and(receives[way], part == 1))
+                    def _(way=way):
+                        rate_x(way, y).wait_recv()
+                        for k in range(3):
+                            first_move(s, k + (0 if way == 0 else 3 + NX), 3 + y)
+
+                moves, gaps = first_slopes(s, y)
+                ax, ay, dt = alpha[0], alpha[1], alpha[2]
+                for x in range(NX):
+                    gap_y = rates[3, 3 + x, pl.ds((3 + y) * SUB, SUB), :]
+                    rate = moves[x] + (ax * gaps[x] + ay * gap_y)
+                    moved = frame[cell(s, 3 + x, 3 + y)] + dt * rate
+                    frame[cell(s + 1, 3 + x, 3 + y)] = (
+                        keep * frame[cell(base, 3 + x, 3 + y)] + take * moved
+                    )
+
+                @pl.when(s < 5)
+                def _():
+                    send_column(s + 1, y)
+                    send_rows(s + 1, i)
+
+            @pl.when(part == 1)
+            def _():
+                finish_rates()
+
+            @pl.when(part == 2)
+            def _():
+                finish_sends(s)
 
         @pl.when(s == 2)
         def _():
             ar_start(1, 0, own_row())
-
-        finish_sends(s)
 
     for x in range(NX):
         for j in range(TILES):
@@ -554,7 +650,7 @@
     most = max(gx_count, gy_count)
     return pl.pallas_call(
         functools.partial(kernel, gx_count, gy_count),
-        out_shape=jax.ShapeDtypeStruct((NX, NY, LANES), jnp.float32),
+        out_shape=pltpu.VMEM((NX, NY, LANES), jnp.float32),
         in_specs=[pl.BlockSpec(memory_space=pl.ANY)] * 3,
         out_specs=pl.BlockSpec(memory_space=pltpu.VMEM),
         scratch_shapes=[
@@ -564,18 +660,19 @@
             pltpu.VMEM((7 * FX, FY * SUB, LANE), jnp.float32),
             pltpu.VMEM((NX, NY * SUB, LANE), jnp.float32),
             pltpu.VMEM((NX, NY * SUB, LANE), jnp.float32),
-            pltpu.VMEM((NX, NY * SUB, LANE), jnp.float32),
-            pltpu.VMEM((NX, NY * SUB, LANE), jnp.float32),
-            pltpu.VMEM((NX, NY * SUB, LANE), jnp.float32),
+            pltpu.VMEM((4, FX, FY * SUB, LANE), jnp.float32),
             pltpu.VMEM((3, SUB, LANE), jnp.float32),
             pltpu.VMEM((2, SUB, LANE), jnp.float32),
             pltpu.VMEM((4, 1, LANE), jnp.float32),
             pltpu.VMEM((4, most - 1, 1, LANE), jnp.float32),
             pltpu.SemaphoreType.DMA((3,)),
-            pltpu.SemaphoreType.DMA((2, 2, NY)),
+            pltpu.SemaphoreType.DMA((2, 2)),
             pltpu.SemaphoreType.DMA((2, 2, NY)),
             pltpu.SemaphoreType.DMA((2, 2)),
             pltpu.SemaphoreType.DMA((2, 2)),
+            pltpu.SemaphoreType.DMA((4,)),
+            pltpu.SemaphoreType.DMA((2,)),
+            pltpu.SemaphoreType.DMA((2, NY)),
             pltpu.SemaphoreType.DMA((4,)),
             pltpu.SemaphoreType.DMA((4,)),
         ],

time: 54 us -> 51.3 us (0.950)
  the two profiles are of different devices: /device:TPU:1 before, /device:TPU:2 now
where the time goes in v3:
time: 51.3 us; the launch traced here: 51.2 us
  Pallas kernels  50.5 us (98%)
  local copies, waits for them, and re-layouts  0.66 us (1%)
    pallas_call x1, Pallas kernels, body(): pl.pallas_call(functools.partial(kernel, gx_count, gy_count), out_shape=p...  50.5 us

profile of v3, /device:TPU:2, one launch (start us, length us, event | category | flops | bytes accessed | tf_op | source)
XLA Modules:
  0.0 51.2 jit_solution(2353886474183666853)
XLA Ops:
  0.0 50.5 %shard_map.37 = f32[4,8,1024]{2,1,0:T(8,128)S(1)} custom-call(f32[4,8,1024]{2,1,0:T(8,128)} %u_hbm.1, f32[4,8]{1,0:T(4,128)} %dist_hbm.1, f32[2,8,128]{2,1,0:T(8,128)} %constant.2.clone.coord_hbm), custom_call_target="tpu_custom_call" | custom-call | tf_op jit(solution)/shard_map/pallas_call | solution.py:651
  50.5 0.7 %copy.5 = f32[4,8,1024]{2,1,0:T(8,128)} copy(f32[4,8,1024]{2,1,0:T(8,128)S(1)} %shard_map.37) | data formatting | bytes 262144

commit v4 on v3

--- a/solution.py
+++ b/solution.py
@@ -19,6 +19,7 @@
 SUB = 8
 LANE = 128
 TILES = LANES // LANE
+PITCH = NY + 1
 FX = NX + 6
 FY = NY + 6
 
@@ -199,6 +200,7 @@
     dist_ref,
     coord_ref,
     frame,
+    turned,
     flat,
     py,
     rates,
@@ -234,7 +236,8 @@
 
         @pl.loop(0, count - 1)
         def _(i, count=count, axis=axis):
-            k = lax.rem(i + count // 3, count - 1) + 1
+            k = i + count // 3 + 1
+            k = jnp.where(k < count, k, k - count + 1)
             where = (lax.rem(gx + k, count), gy) if axis == 0 else (gx, lax.rem(gy + k, count))
             pl.semaphore_signal(barrier, inc=1, device_id=where, device_id_type=MESH)
 
@@ -249,13 +252,15 @@
     for x in range(NX):
         for j in range(TILES):
             tile = u_ref[x, :, j * LANE : (j + 1) * LANE]
-            frame[3 + x, pl.ds(3 * SUB + j, SUB, stride=SUB), :] = SCALE * tile
-
-    def flat_pass(s):
+            turned[x, pl.ds(j * PITCH, NY), :] = SCALE * tile
+    for x in range(NX):
+        for y in range(NY):
+            frame[cell(0, 3 + x, 3 + y)] = turned[x, pl.ds(y, SUB, stride=PITCH), :]
+
+    def flat_pass():
         @pl.loop(0, NX)
         def _(x):
-            row = s * FX + 3 + x
-            tiles = [frame[row, pl.ds(3 * SUB + j, SUB, stride=SUB), :] for j in range(TILES)]
+            tiles = [turned[x, pl.ds(j * PITCH, NY), :] for j in range(TILES)]
             parts = [None] * TILES
             for j in range(TILES):
                 total, gap = heading_slopes(tiles[j], lane)
@@ -272,7 +277,7 @@
                 for c in range(TURNS):
                     parts[2 * c + k] += (torque / (12.0 * step_xy)) * (gaps[c] - jnp.abs(sums[c]))
             for j in range(TILES):
-                flat[x, pl.ds(j, SUB, stride=SUB), :] = parts[j]
+                flat[x, pl.ds(j * PITCH, NY), :] = parts[j]
 
     sends = (gx < gx_count - 1, gx > 0, gy < gy_count - 1, gy > 0)
     receives = (gx > 0, gx < gx_count - 1, gy > 0, gy < gy_count - 1)
@@ -305,21 +310,19 @@
     def column(i):
         return jnp.where(i < 3, i, jnp.where(i < 6, i + 2, i - 3))
 
-    def send_column(s, y):
+    def send_column(s, y, when=True):
         for way in range(2):
 
-            @pl.when(sends[way])
+            @pl.when(jnp.logical_and(sends[way], when))
             def _(way=way):
                 halo_x(s, way, y).start()
 
-    def send_rows(s, i):
-        @pl.when(jnp.logical_and(i == 2, sends[3]))
-        def _():
-            halo_y(s, 1).start()
-
-        @pl.when(jnp.logical_and(i == 5, sends[2]))
-        def _():
-            halo_y(s, 0).start()
+    def send_rows(s, i, when=True):
+        for way, last in ((1, 2), (0, 5)):
+
+            @pl.when(jnp.logical_and(jnp.logical_and(i == last, sends[2 + way]), when))
+            def _(way=way):
+                halo_y(s, way).start()
 
     def finish_sends(s):
         turn = lax.rem(s, 2)
@@ -397,10 +400,13 @@
             def _(way=way):
                 rate_y(way).wait_send()
 
-    def first_move(s, x, y):
+    def first_moved(s, x, y):
         at = pl.ds(y * SUB, SUB)
         rate = rates[0, x, at, :] + (alpha[0] * rates[1, x, at, :] + alpha[1] * rates[2, x, at, :])
-        frame[cell(s, x, y)] = frame[cell(s - 1, x, y)] + alpha[2] * rate
+        return frame[cell(s - 1, x, y)] + alpha[2] * rate
+
+    def first_move(s, x, y):
+        frame[cell(s, x, y)] = first_moved(s, x, y)
 
     def fill_ghosts(s):
         for low, outside in ((True, gx == 0), (False, gx == gx_count - 1)):
@@ -429,16 +435,16 @@
                     for k in (1, 2, 3):
                         frame[cell(s, 3 + x, end + step * k)] = edge + float(k) * slope
 
-    def second_pass(s, part):
-        slot = jnp.where(part == 0, 2, 3)
+    def second_pass(s, third):
+        slot = jnp.where(third == 0, 2, 3)
 
         for way in range(2):
 
-            @pl.when(jnp.logical_and(receives[2 + way], part != 1))
+            @pl.when(jnp.logical_and(receives[2 + way], third != 1))
             def _(way=way):
                 halo_y(s, way).wait_recv()
 
-            @pl.when(jnp.logical_and(receives[2 + way], part == 1))
+            @pl.when(jnp.logical_and(receives[2 + way], third == 1))
             def _(way=way):
                 rate_y(way).wait_recv()
 
@@ -469,7 +475,7 @@
             top_x = jnp.maximum(top_x, jnp.abs(vx - pull * sx))
             top_y = jnp.maximum(top_y, jnp.abs(vy - pull * sy))
             moves.append(
-                flat[at] + (1.0 / (12.0 * step_xy)) * ((pull * square) - (sx * vx + sy * vy))
+                flat[x, pl.ds(y, SUB, stride=PITCH), :] + (1.0 / (12.0 * step_xy)) * ((pull * square) - (sx * vx + sy * vy))
             )
         peak[0] = top_x
         peak[1] = top_y
@@ -483,8 +489,8 @@
         return jnp.maximum(v, pltpu.roll(v, LANE // 2, 1))
 
     def ar_copy(turn, phase, k):
-        count = gy_count if phase == 0 else gx_count
-        where = (gx, lax.rem(gy + k, count)) if phase == 0 else (lax.rem(gx + k, count), gy)
+        count = gy_count if phase == 1 else gx_count
+        where = (gx, lax.rem(gy + k, count)) if phase == 1 else (lax.rem(gx + k, count), gy)
         return pltpu.make_async_remote_copy(
             src_ref=arsend.at[2 * turn + phase],
             dst_ref=arrecv.at[2 * turn + phase, k - 1],
@@ -497,14 +503,15 @@
     def ar_start(turn, phase, row):
         arsend[2 * turn + phase] = row
 
-        count = gy_count if phase == 0 else gx_count
+        count = gy_count if phase == 1 else gx_count
 
         @pl.loop(0, count - 1)
         def _(i):
-            ar_copy(turn, phase, lax.rem(i + count // 3, count - 1) + 1).start()
+            k = i + count // 3 + 1
+            ar_copy(turn, phase, jnp.where(k < count, k, k - count + 1)).start()
 
     def ar_finish(turn, phase):
-        count = gy_count if phase == 0 else gx_count
+        count = gy_count if phase == 1 else gx_count
         slot = 2 * turn + phase
         every = arrecv.at[slot, pl.ds(0, count - 1)]
         whole = pltpu.make_async_remote_copy(
@@ -547,18 +554,14 @@
 
     @pl.loop(0, 6)
     def _(s):
-        part = lax.rem(s, 3)
-        base = s - part
-
-        flat_pass(s)
+        third = lax.rem(s, 3)
+        base = s - third
+
+        flat_pass()
         fill_ghosts(s)
-        second_pass(s, part)
-
-        @pl.when(s == 3)
-        def _():
-            ar_start(1, 1, ar_finish(1, 0))
-
-        @pl.when(part == 0)
+        second_pass(s, third)
+
+        @pl.when(third == 0)
         def _():
             @pl.loop(0, NY)
             def _(i):
@@ -573,68 +576,92 @@
                 for x in range(NX):
                     rates[0, 3 + x, pl.ds((3 + y) * SUB, SUB), :] = moves[x]
                     rates[1, 3 + x, pl.ds((3 + y) * SUB, SUB), :] = gaps[x]
-                send_rates(i, y)
+
+                @pl.when(jnp.logical_and(s == 3, i < 3))
+                def _():
+                    send_rates(i, y)
 
             @pl.when(s == 0)
             def _():
                 ar_start(0, 0, own_row())
+
+                @pl.loop(0, NY)
+                def _(i):
+                    send_rates(i, column(i))
+
                 ar_start(0, 1, ar_finish(0, 0))
                 set_alpha(ar_finish(0, 1))
                 peak[...] = jnp.zeros_like(peak)
 
             @pl.when(s == 3)
             def _():
+                ar_start(1, 1, ar_finish(1, 0))
+
+                @pl.loop(3, NY)
+                def _(i):
+                    send_rates(i, column(i))
+
                 set_alpha(ar_finish(1, 1))
 
             @pl.loop(0, NY)
             def _(y):
                 for x in range(NX):
-                    first_move(s + 1, 3 + x, 3 + y)
+                    following = first_moved(s + 1, 3 + x, 3 + y)
+                    frame[cell(s + 1, 3 + x, 3 + y)] = following
+                    turned[x, pl.ds(y, SUB, stride=PITCH), :] = following
 
             finish_sends(s)
 
-        @pl.when(part > 0)
+        def advance(y, keep, take):
+            moves, gaps = first_slopes(s, y)
+            ax, ay, dt = alpha[0], alpha[1], alpha[2]
+            for x in range(NX):
+                gap_y = rates[3, 3 + x, pl.ds((3 + y) * SUB, SUB), :]
+                rate = moves[x] + (ax * gaps[x] + ay * gap_y)
+                moved = frame[cell(s, 3 + x, 3 + y)] + dt * rate
+                following = keep * frame[cell(base, 3 + x, 3 + y)] + take * moved
+                frame[cell(s + 1, 3 + x, 3 + y)] = following
+                turned[x, pl.ds(y, SUB, stride=PITCH), :] = following
+
+        @pl.when(third == 1)
         def _():
-            keep = jnp.where(part == 1, 0.75, 1.0 / 3.0)
-            take = jnp.where(part == 1, 0.25, 2.0 / 3.0)
-
             @pl.loop(0, NY)
             def _(i):
                 y = column(i)
                 for way in range(2):
 
-                    @pl.when(jnp.logical_and(receives[way], part == 2))
+                    @pl.when(receives[way])
+                    def _(way=way):
+                        rate_x(way, y).wait_recv()
+
+                for way in range(2):
+                    for k in range(3):
+                        x = k + (0 if way == 0 else 3 + NX)
+                        frame[cell(s, x, 3 + y)] = jnp.where(
+                            receives[way], first_moved(s, x, 3 + y), frame[cell(s, x, 3 + y)]
+                        )
+                advance(y, 0.75, 0.25)
+                send_column(s + 1, y)
+                send_rows(s + 1, i)
+
+            finish_rates()
+
+        @pl.when(third == 2)
+        def _():
+            @pl.loop(0, NY)
+            def _(i):
+                y = column(i)
+                for way in range(2):
+
+                    @pl.when(receives[way])
                     def _(way=way):
                         halo_x(s, way, y).wait_recv()
 
-                    @pl.when(jnp.logical_and(receives[way], part == 1))
-                    def _(way=way):
-                        rate_x(way, y).wait_recv()
-                        for k in range(3):
-                            first_move(s, k + (0 if way == 0 else 3 + NX), 3 + y)
-
-                moves, gaps = first_slopes(s, y)
-                ax, ay, dt = alpha[0], alpha[1], alpha[2]
-                for x in range(NX):
-                    gap_y = rates[3, 3 + x, pl.ds((3 + y) * SUB, SUB), :]
-                    rate = moves[x] + (ax * gaps[x] + ay * gap_y)
-                    moved = frame[cell(s, 3 + x, 3 + y)] + dt * rate
-                    frame[cell(s + 1, 3 + x, 3 + y)] = (
-                        keep * frame[cell(base, 3 + x, 3 + y)] + take * moved
-                    )
-
-                @pl.when(s < 5)
-                def _():
-                    send_column(s + 1, y)
-                    send_rows(s + 1, i)
-
-            @pl.when(part == 1)
-            def _():
-                finish_rates()
-
-            @pl.when(part == 2)
-            def _():
-                finish_sends(s)
+                advance(y, 1.0 / 3.0, 2.0 / 3.0)
+                send_column(s + 1, y, s < 5)
+                send_rows(s + 1, i, s < 5)
+
+            finish_sends(s)
 
         @pl.when(s == 2)
         def _():
@@ -642,7 +669,7 @@
 
     for x in range(NX):
         for j in range(TILES):
-            tile = frame[6 * FX + 3 + x, pl.ds(3 * SUB + j, SUB, stride=SUB), :]
+            tile = turned[x, pl.ds(j * PITCH, NY), :]
             out_ref[x, :, j * LANE : (j + 1) * LANE] = (1.0 / SCALE) * tile
 
 
@@ -658,7 +685,8 @@
             pltpu.SMEM((NX, NY), jnp.float32),
             pltpu.VMEM((2, SUB, LANE), jnp.float32),
             pltpu.VMEM((7 * FX, FY * SUB, LANE), jnp.float32),
-            pltpu.VMEM((NX, NY * SUB, LANE), jnp.float32),
+            pltpu.VMEM((NX, TILES * PITCH, LANE), jnp.float32),
+            pltpu.VMEM((NX, TILES * PITCH, LANE), jnp.float32),
             pltpu.VMEM((NX, NY * SUB, LANE), jnp.float32),
             pltpu.VMEM((4, FX, FY * SUB, LANE), jnp.float32),
             pltpu.VMEM((3, SUB, LANE), jnp.float32),

time: 51.3 us -> 49.8 us (0.971)
  the two profiles are of different devices: /device:TPU:2 before, /device:TPU:1 now
where the time goes in v4:
time: 49.8 us; the launch traced here: 49.7 us
  Pallas kernels  49.1 us (99%)
  local copies, waits for them, and re-layouts  0.66 us (1%)
    pallas_call x1, Pallas kernels, body(): pl.pallas_call(functools.partial(kernel, gx_count, gy_count), out_shape=p...  49.1 us

profile of v4, /device:TPU:1, one launch (start us, length us, event | category | flops | bytes accessed | tf_op | source)
XLA Modules:
  0.0 49.7 jit_solution(13889527247044963026)
XLA Ops:
  0.0 49.1 %shard_map.37 = f32[4,8,1024]{2,1,0:T(8,128)S(1)} custom-call(f32[4,8,1024]{2,1,0:T(8,128)} %u_hbm.1, f32[4,8]{1,0:T(4,128)} %dist_hbm.1, f32[2,8,128]{2,1,0:T(8,128)} %constant.2.clone.coord_hbm), custom_call_target="tpu_custom_call" | custom-call | tf_op jit(solution)/shard_map/pallas_call | solution.py:678
  49.1 0.7 %copy.5 = f32[4,8,1024]{2,1,0:T(8,128)} copy(f32[4,8,1024]{2,1,0:T(8,128)S(1)} %shard_map.37) | data formatting | bytes 262144

commit v5 on v4

--- a/solution.py
+++ b/solution.py
@@ -310,17 +310,17 @@
     def column(i):
         return jnp.where(i < 3, i, jnp.where(i < 6, i + 2, i - 3))
 
-    def send_column(s, y, when=True):
+    def send_column(s, y):
         for way in range(2):
 
-            @pl.when(jnp.logical_and(sends[way], when))
+            @pl.when(sends[way])
             def _(way=way):
                 halo_x(s, way, y).start()
 
-    def send_rows(s, i, when=True):
+    def send_rows(s, i):
         for way, last in ((1, 2), (0, 5)):
 
-            @pl.when(jnp.logical_and(jnp.logical_and(i == last, sends[2 + way]), when))
+            @pl.when(jnp.logical_and(i == last, sends[2 + way]))
             def _(way=way):
                 halo_y(s, way).start()
 
@@ -366,20 +366,19 @@
             device_id_type=MESH,
         )
 
-    def send_rates(i, y):
+    def send_rates(y):
         for way in range(2):
 
             @pl.when(sends[way])
             def _(way=way):
                 rate_x(way, y).start()
 
-        @pl.when(jnp.logical_and(i == 2, sends[3]))
-        def _():
-            rate_y(1).start()
-
-        @pl.when(jnp.logical_and(i == 5, sends[2]))
-        def _():
-            rate_y(0).start()
+    def send_rate_rows():
+        for way in range(2):
+
+            @pl.when(sends[2 + way])
+            def _(way=way):
+                rate_y(way).start()
 
     def finish_rates():
         every = rates.at[pl.ds(0, 3), pl.ds(0, 3), pl.ds(3 * SUB, NY * SUB)]
@@ -579,15 +578,17 @@
 
                 @pl.when(jnp.logical_and(s == 3, i < 3))
                 def _():
-                    send_rates(i, y)
+                    send_rates(y)
 
             @pl.when(s == 0)
             def _():
                 ar_start(0, 0, own_row())
 
+                send_rate_rows()
+
                 @pl.loop(0, NY)
                 def _(i):
-                    send_rates(i, column(i))
+                    send_rates(column(i))
 
                 ar_start(0, 1, ar_finish(0, 0))
                 set_alpha(ar_finish(0, 1))
@@ -597,9 +598,11 @@
             def _():
                 ar_start(1, 1, ar_finish(1, 0))
 
+                send_rate_rows()
+
                 @pl.loop(3, NY)
                 def _(i):
-                    send_rates(i, column(i))
+                    send_rates(column(i))
 
                 set_alpha(ar_finish(1, 1))
 
@@ -658,14 +661,17 @@
                         halo_x(s, way, y).wait_recv()
 
                 advance(y, 1.0 / 3.0, 2.0 / 3.0)
-                send_column(s + 1, y, s < 5)
-                send_rows(s + 1, i, s < 5)
 
             finish_sends(s)
 
         @pl.when(s == 2)
         def _():
             ar_start(1, 0, own_row())
+
+            @pl.loop(0, NY)
+            def _(i):
+                send_column(s + 1, column(i))
+                send_rows(s + 1, i)
 
     for x in range(NX):
         for j in range(TILES):

time: 49.8 us -> 49.3 us (0.990)
  Pallas kernels: 49.1 us -> 48.5 us
    pallas_call x1, Pallas kernels: 49.1 us -> 48.5 us  [body(): pl.pallas_call(functools.partial(kernel, gx_count, gy_count), out_shape=p...]
where the time goes in v5:
time: 49.3 us; the launch traced here: 49.2 us
  Pallas kernels  48.5 us (98%)
  local copies, waits for them, and re-layouts  0.66 us (1%)
    pallas_call x1, Pallas kernels, body(): pl.pallas_call(functools.partial(kernel, gx_count, gy_count), out_shape=p...  48.5 us

profile of v5, /device:TPU:1, one launch (start us, length us, event | category | flops | bytes accessed | tf_op | source)
XLA Modules:
  0.0 49.2 jit_solution(13604819596220226656)
XLA Ops:
  0.0 48.5 %shard_map.37 = f32[4,8,1024]{2,1,0:T(8,128)S(1)} custom-call(f32[4,8,1024]{2,1,0:T(8,128)} %u_hbm.1, f32[4,8]{1,0:T(4,128)} %dist_hbm.1, f32[2,8,128]{2,1,0:T(8,128)} %constant.2.clone.coord_hbm), custom_call_target="tpu_custom_call" | custom-call | tf_op jit(solution)/shard_map/pallas_call | solution.py:684
  48.5 0.7 %copy.5 = f32[4,8,1024]{2,1,0:T(8,128)} copy(f32[4,8,1024]{2,1,0:T(8,128)S(1)} %shard_map.37) | data formatting | bytes 262144

commit v6 on v5

--- a/solution.py
+++ b/solution.py
@@ -662,6 +662,10 @@
 
                 advance(y, 1.0 / 3.0, 2.0 / 3.0)
 
+                @pl.when(jnp.logical_and(s == 2, i < 4))
+                def _():
+                    send_column(s + 1, y)
+
             finish_sends(s)
 
         @pl.when(s == 2)
@@ -670,8 +674,11 @@
 
             @pl.loop(0, NY)
             def _(i):
+                send_rows(s + 1, i)
+
+            @pl.loop(4, NY)
+            def _(i):
                 send_column(s + 1, column(i))
-                send_rows(s + 1, i)
 
     for x in range(NX):
         for j in range(TILES):
@@ -691,8 +698,8 @@
             pltpu.SMEM((NX, NY), jnp.float32),
             pltpu.VMEM((2, SUB, LANE), jnp.float32),
             pltpu.VMEM((7 * FX, FY * SUB, LANE), jnp.float32),
-            pltpu.VMEM((NX, TILES * PITCH, LANE), jnp.float32),
-            pltpu.VMEM((NX, TILES * PITCH, LANE), jnp.float32),
+            pltpu.VMEM((NX, (TILES + 1) * PITCH - 1, LANE), jnp.float32),
+            pltpu.VMEM((NX, (TILES + 1) * PITCH - 1, LANE), jnp.float32),
             pltpu.VMEM((NX, NY * SUB, LANE), jnp.float32),
             pltpu.VMEM((4, FX, FY * SUB, LANE), jnp.float32),
             pltpu.VMEM((3, SUB, LANE), jnp.float32),

time: 49.3 us -> 49.3 us (level)
  no operation moved by 1% of the time
where the time goes in v6:
time: 49.3 us; the launch traced here: 49.2 us
  Pallas kernels  48.6 us (99%)
  local copies, waits for them, and re-layouts  0.66 us (1%)
    pallas_call x1, Pallas kernels, body(): pl.pallas_call(functools.partial(kernel, gx_count, gy_count), out_shape=p...  48.6 us

profile of v6, /device:TPU:1, one launch (start us, length us, event | category | flops | bytes accessed | tf_op | source)
XLA Modules:
  0.0 49.2 jit_solution(13074156285216906061)
XLA Ops:
  0.0 48.6 %shard_map.37 = f32[4,8,1024]{2,1,0:T(8,128)S(1)} custom-call(f32[4,8,1024]{2,1,0:T(8,128)} %u_hbm.1, f32[4,8]{1,0:T(4,128)} %dist_hbm.1, f32[2,8,128]{2,1,0:T(8,128)} %constant.2.clone.coord_hbm), custom_call_target="tpu_custom_call" | custom-call | tf_op jit(solution)/shard_map/pallas_call | solution.py:691
  48.6 0.7 %copy.5 = f32[4,8,1024]{2,1,0:T(8,128)} copy(f32[4,8,1024]{2,1,0:T(8,128)S(1)} %shard_map.37) | data formatting | bytes 262144
